TPU v7x, 512 devices: a whole 4x8x8 slice. The times are simulated.
512 devices in a mesh: tok: 32 (over y, x), exp: 16 (over z, core).
Axes of the slice: x: 4, y: 8, z: 8, core: 2. Of those that a mesh axis runs over, the one named last changes fastest.
Arguments:
- tokens: bfloat16 [512, 6144], P('tok', 'exp'), may hold values from -6 to 6
- route_ids: int32 [512, 2], P('tok'), may hold values from 0 to 3, all different within a row; in each aligned block of 16 rows (0 to 15, 16 to 31, ...) at most 12 rows name the same one
- gate_codes: int32 [512, 2], P('tok'), may hold values from 1 to 255
- merge_labels: int32 [4], replicated, may hold values from 0 to 1, as said below
- freq_counts: int32 [4], replicated, may hold values from 1024 to 4096
- w_gate: bfloat16 [32768, 6144], P(('tok', 'exp')), may hold values from -0.078125 to 0.078125
- w_up: bfloat16 [32768, 6144], P(('tok', 'exp')), may hold values from -0.078125 to 0.078125
- w_down: bfloat16 [32768, 6144], P('tok', 'exp'), may hold values from -0.0625 to 0.0625
Outputs:
- initial_out: bfloat16 [512, 6144], P('tok', 'exp')
- merged_out: bfloat16 [512, 6144], P('tok', 'exp')
Inputs may be any that keep to these rules, and one draw needn't show every extreme that they name: `route_ids`: the 2 ids of a row differ. Among the 16 rows of one token shard no expert is named more than 12 times, a bound that some block reaches. `merge_labels`: experts with equal labels form one merge group; every group has exactly two experts.
All inputs are finite; a program needn't handle non-finite values.
Results may differ from a plain program's by a relative error of at most 0.0085.
Values may be sent and summed in bfloat16 or wider, within the bound.
A program may use at most 64 MiB of HBM per device.

v0:
```python
import jax
import jax.numpy as jnp
from jax import lax
from jax.sharding import PartitionSpec as P

EXPERTS = 4
TOP = 2
CAP = 12


def passed_along(value, axis, by):
    devices = lax.axis_size(axis)
    return lax.ppermute(value, axis, [(i, (i + by) % devices) for i in range(devices)])


def local(tokens, route_ids, gate_codes, merge_labels, freq_counts, w_gate, w_up, w_down):
    n_tok = lax.axis_size("tok")
    span = n_tok // EXPERTS
    expert = lax.axis_index("tok") // span
    tok_dev = tokens.shape[0]
    width = tokens.shape[1]
    flat = route_ids.reshape(-1)
    labels_idx = jnp.arange(EXPERTS, dtype=jnp.int32)
    picked = (flat[:, None] == labels_idx[None, :]).astype(jnp.int32)
    before = jnp.cumsum(picked, axis=0) - picked
    slot = jnp.sum(before * picked, axis=1)
    places = jnp.arange(CAP, dtype=jnp.int32)
    landing = picked.T[:, None, :] * (slot[None, None, :] == places[None, :, None]).astype(
        jnp.int32
    )
    landing = landing.reshape(EXPERTS, CAP, tok_dev, TOP)
    scale = gate_codes.astype(jnp.float32) / 256.0
    place_map = jnp.sum(landing, axis=3).astype(jnp.bfloat16)
    weighted = jnp.sum(landing.astype(jnp.float32) * scale[None, None, :, :], axis=3)
    packed = jnp.einsum(
        "ecn,nd->ecd", place_map, tokens, preferred_element_type=jnp.float32
    ).astype(jnp.bfloat16)
    copies = jnp.repeat(packed, span, axis=0)
    arrived = lax.all_to_all(copies, "tok", split_axis=0, concat_axis=0, tiled=True)
    rows_part = arrived.reshape(n_tok * CAP, width)
    rows = lax.all_gather(rows_part, "exp", axis=1, tiled=True)

    def project(gate_w, up_w, down_w):
        gate = jnp.einsum("sd,fd->sf", rows, gate_w, preferred_element_type=jnp.float32)
        upper = jnp.einsum("sd,fd->sf", rows, up_w, preferred_element_type=jnp.float32)
        hidden = (jax.nn.silu(gate) * upper).astype(jnp.bfloat16)
        units = lax.all_gather(hidden, "exp", axis=1, tiled=True)
        return jnp.dot(units, down_w, preferred_element_type=jnp.float32)

    first = project(w_gate, w_up, w_down)
    freq = freq_counts.astype(jnp.float32)
    own_label = jnp.sum(jnp.where(labels_idx == expert, merge_labels, 0))
    member = jnp.where(merge_labels == own_label, freq, jnp.float32(0.0))
    coef = member / jnp.sum(member)

    def weight_of(source):
        return jnp.sum(jnp.where(labels_idx == source, coef, jnp.float32(0.0)))

    own_weight = weight_of(expert)
    accums = (
        own_weight * w_gate.astype(jnp.float32),
        own_weight * w_up.astype(jnp.float32),
        own_weight * w_down.astype(jnp.float32),
    )
    for offset in range(1, EXPERTS):
        peers = passed_along((w_gate, w_up, w_down), "tok", offset * span)
        factor = weight_of((expert - offset) % EXPERTS)
        accums = (
            accums[0] + factor * peers[0].astype(jnp.float32),
            accums[1] + factor * peers[1].astype(jnp.float32),
            accums[2] + factor * peers[2].astype(jnp.float32),
        )
    second = project(
        accums[0].astype(jnp.bfloat16),
        accums[1].astype(jnp.bfloat16),
        accums[2].astype(jnp.bfloat16),
    )
    stacked = jnp.stack(
        [first.reshape(n_tok, CAP, width), second.reshape(n_tok, CAP, width)], axis=0
    )
    backs = lax.all_to_all(
        stacked.astype(jnp.bfloat16), "tok", split_axis=1, concat_axis=1, tiled=True
    ).astype(stacked.dtype)
    totals = jnp.sum(backs.reshape(2, EXPERTS, span, CAP, width), axis=2)
    final = jnp.einsum(
        "ecn,xecd->xnd",
        weighted,
        totals,
        precision=lax.Precision.HIGHEST,
        preferred_element_type=jnp.float32,
    )
    return (final[0].astype(jnp.bfloat16), final[1].astype(jnp.bfloat16))


def solution(mesh):
    return jax.shard_map(
        local,
        mesh=mesh,
        in_specs=(
            P("tok", "exp"),
            P("tok", None),
            P("tok", None),
            P(),
            P(),
            P(("tok", "exp"), None),
            P(("tok", "exp"), None),
            P("tok", "exp"),
        ),
        out_specs=(P("tok", "exp"), P("tok", "exp")),
        check_vma=False,
    )
```

profile of v0, /device:TPU:1, one launch (start us, length us, event | category | flops | bytes accessed | tf_op | source)
XLA Modules:
  0.0 293.7 jit_solution(11261646485899905770)
XLA Ops:
  7.2 0.0 copy-start
  7.2 0.0 all-gather.2.cloned.1.call-start
  7.3 0.8 fusion.23
  8.1 0.8 copy.25
  8.8 0.1 eq.85
  8.9 0.1 fusion.21
  9.0 0.1 reduce_window_sum.11
  9.0 0.2 select_reduce_fusion
  9.2 0.1 eq.89
  9.3 0.1 copy.26
  9.5 0.1 convolution_convert_fusion.2
  9.6 24.1 %all_to_all.10 = bf16[32,12,384]{2,1,0:T(8,128)(2,1)S(1)} all-to-all(bf16[32,12,384]{2,1,0:T(8,128)(2,1)S(1)} %bitcast.34), channel_id=1, replica_groups=mesh['tok'=32,'exp'=16] {'tok'}, dimensions={0} | all-to-all | bytes 589824 | tf_op jit(solution)/shard_map/all_to_all | solution.py:39
  33.8 0.8 reshape.75
  34.5 0.0 all-gather.2.cloned.1.call-update
  34.6 3.7 %collective-permute-start = (bf16[64,6144]{1,0:T(8,128)(2,1)S(1)}, bf16[64,6144]{1,0:T(8,128)(2,1)}, u32[]{:S(2)}, u32[]{:S(2)}) collective-permute-start(bf16[64,6144]{1,0:T(8,128)(2,1)S(1)} %copy-done.2), channel_id=1, source_target_pairs={{0,128},{16,144},{32,160},{48,176},{64,192},{80,208},{96,224},{112... | collective-permute-start | bytes 2359304 | tf_op jit(solution)/shard_map/ppermute | solution.py:13
  38.3 3.7 %collective-permute-start.2 = (bf16[64,6144]{1,0:T(8,128)(2,1)S(1)}, bf16[64,6144]{1,0:T(8,128)(2,1)}, u32[]{:S(2)}, u32[]{:S(2)}) collective-permute-start(bf16[64,6144]{1,0:T(8,128)(2,1)S(1)} %copy-done.2), channel_id=1, source_target_pairs={{0,384},{16,400},{32,416},{48,432},{64,448},{80,464},{96,480},{112... | collective-permute-start | bytes 2359304 | tf_op jit(solution)/shard_map/ppermute | solution.py:13
  42.0 3.5 %collective-permute-start.1 = (bf16[64,6144]{1,0:T(8,128)(2,1)S(1)}, bf16[64,6144]{1,0:T(8,128)(2,1)}, u32[]{:S(2)}, u32[]{:S(2)}) collective-permute-start(bf16[64,6144]{1,0:T(8,128)(2,1)S(1)} %copy-done.2), channel_id=1, source_target_pairs={{0,256},{16,272},{32,288},{48,304},{64,320},{80,336},{96,352},{112... | collective-permute-start | bytes 2359304 | tf_op jit(solution)/shard_map/ppermute | solution.py:13
  45.5 3.0 %collective-permute-start.3 = (bf16[64,6144]{1,0:T(8,128)(2,1)S(1)}, bf16[64,6144]{1,0:T(8,128)(2,1)}, u32[]{:S(2)}, u32[]{:S(2)}) collective-permute-start(bf16[64,6144]{1,0:T(8,128)(2,1)S(1)} %copy-done.3), channel_id=1, source_target_pairs={{0,128},{16,144},{32,160},{48,176},{64,192},{80,208},{96,224},{112... | collective-permute-start | bytes 2359304 | tf_op jit(solution)/shard_map/ppermute | solution.py:13
  48.5 4.4 %collective-permute-start.5 = (bf16[64,6144]{1,0:T(8,128)(2,1)S(1)}, bf16[64,6144]{1,0:T(8,128)(2,1)}, u32[]{:S(2)}, u32[]{:S(2)}) collective-permute-start(bf16[64,6144]{1,0:T(8,128)(2,1)S(1)} %copy-done.3), channel_id=1, source_target_pairs={{0,384},{16,400},{32,416},{48,432},{64,448},{80,464},{96,480},{112... | collective-permute-start | bytes 2359304 | tf_op jit(solution)/shard_map/ppermute | solution.py:13
  53.0 0.6 fusion.24
  53.7 1.2 fusion.29
  54.9 2.0 fusion.25
  56.9 25.6 %all-gather.2.cloned.1.call-done = bf16[384,6144]{1,0:T(8,128)(2,1)} async-done(((bf16[384,384]{1,0:T(8,128)(2,1)}), bf16[384,6144]{1,0:T(8,128)(2,1)}) %all-gather.2.cloned.1.call-update) | async-done | bytes 4718608 | tf_op jit(solution)/shard_map/all_gather | solution.py:41
  82.5 4.1 %fusion.30 = f32[384,64]{0,1:T(8,128)S(1)} fusion(bf16[384,6144]{1,0:T(8,128)(2,1)} %all-gather.2.cloned.1.call-done, bf16[64,6144]{1,0:T(8,128)(2,1)S(1)} %copy-done.2), kind=kOutput, calls=%fused_computation.57 | convolution fusion | flops 301989888 | bytes 5603328 | tf_op jit(solution)/shard_map/sd,fd->sf/dot_general | solution.py:44
  86.6 0.0 copy-start.7
  86.6 1.6 fusion
  88.2 18.2 %all_gather.10 = bf16[384,1024]{0,1:T(8,128)(2,1)S(1)} all-gather(bf16[384,64]{0,1:T(8,128)(2,1)S(1)} %fusion), channel_id=1, replica_groups=mesh['tok'=32,'exp'=16] {'exp'}, dimensions={1}, use_global_device_ids=true | all-gather | bytes 835584 | tf_op jit(solution)/shard_map/all_gather | solution.py:47
  106.4 7.0 %collective-permute-start.4 = (bf16[64,6144]{1,0:T(8,128)(2,1)S(1)}, bf16[64,6144]{1,0:T(8,128)(2,1)}, u32[]{:S(2)}, u32[]{:S(2)}) collective-permute-start(bf16[64,6144]{1,0:T(8,128)(2,1)S(1)} %copy-done.3), channel_id=1, source_target_pairs={{0,256},{16,272},{32,288},{48,304},{64,320},{80,336},{96,352},{112... | collective-permute-start | bytes 2359304 | tf_op jit(solution)/shard_map/ppermute | solution.py:13
  113.4 0.6 convolution_convert_fusion.1
  114.0 0.1 stack_reshape.8
  114.1 28.1 %collective-permute-done.2 = bf16[64,6144]{1,0:T(8,128)(2,1)} collective-permute-done((bf16[64,6144]{1,0:T(8,128)(2,1)S(1)}, bf16[64,6144]{1,0:T(8,128)(2,1)}, u32[]{:S(2)}, u32[]{:S(2)}) %collective-permute-start.2) | collective-permute-done | bytes 786464 | tf_op jit(solution)/shard_map/ppermute | solution.py:13
  142.1 4.1 %collective-permute-start.6 = (bf16[1024,384]{1,0:T(8,128)(2,1)}, bf16[1024,384]{1,0:T(8,128)(2,1)S(1)}, u32[]{:S(2)}, u32[]{:S(2)}) collective-permute-start(bf16[1024,384]{1,0:T(8,128)(2,1)} %param.15), channel_id=1, source_target_pairs={{0,128},{16,144},{32,160},{48,176},{64,192},{80,208},{96,224},{112... | collective-permute-start | bytes 2359304 | tf_op jit(solution)/shard_map/ppermute | solution.py:13
  146.3 3.3 %collective-permute-start.8 = (bf16[1024,384]{1,0:T(8,128)(2,1)}, bf16[1024,384]{1,0:T(8,128)(2,1)S(1)}, u32[]{:S(2)}, u32[]{:S(2)}) collective-permute-start(bf16[1024,384]{1,0:T(8,128)(2,1)} %param.15), channel_id=1, source_target_pairs={{0,384},{16,400},{32,416},{48,432},{64,448},{80,464},{96,480},{112... | collective-permute-start | bytes 2359304 | tf_op jit(solution)/shard_map/ppermute | solution.py:13
  149.6 7.7 %fusion.3 = f32[384,64]{0,1:T(8,128)S(1)} fusion(bf16[384,6144]{1,0:T(8,128)(2,1)} %all-gather.2.cloned.1.call-done, bf16[64,6144]{1,0:T(8,128)(2,1)} %collective-permute-done.2, bf16[64,6144]{1,0:T(8,128)(2,1)} %collective-permute-done.1, bf16[64,6144]{1,0:T(8,128)(2,1)} %collective-permute-done, bf16[64,6144]{1,0:T(8,128)(2,1)S(1)} %copy-done.2, ...), kind=kOutput, calls=%fused_computation.12 | convolution fusion | flops 306708480 | bytes 7962640 | tf_op jit(solution)/shard_map/sd,fd->sf/dot_general | solution.py:44
  157.3 5.7 %collective-permute-start.7 = (bf16[1024,384]{1,0:T(8,128)(2,1)S(1)}, bf16[1024,384]{1,0:T(8,128)(2,1)S(1)}, u32[]{:S(2)}, u32[]{:S(2)}) collective-permute-start(bf16[1024,384]{1,0:T(8,128)(2,1)S(1)} %copy-done.8), channel_id=1, source_target_pairs={{0,256},{16,272},{32,288},{48,304},{64,320},{80,336},{96,352},{112... | collective-permute-start | bytes 2359304 | tf_op jit(solution)/shard_map/ppermute | solution.py:13
  163.0 17.4 %collective-permute-done.5 = bf16[64,6144]{1,0:T(8,128)(2,1)} collective-permute-done((bf16[64,6144]{1,0:T(8,128)(2,1)S(1)}, bf16[64,6144]{1,0:T(8,128)(2,1)}, u32[]{:S(2)}, u32[]{:S(2)}) %collective-permute-start.5) | collective-permute-done | bytes 786464 | tf_op jit(solution)/shard_map/ppermute | solution.py:13
  180.4 5.9 %multiply_convert_fusion = bf16[384,64]{0,1:T(8,128)(2,1)S(1)} fusion(f32[384,64]{0,1:T(8,128)S(1)} %fusion.3, bf16[384,6144]{1,0:T(8,128)(2,1)S(1)} %bitcast.33, bf16[64,6144]{1,0:T(8,128)(2,1)} %collective-permute-done.5, bf16[64,6144]{1,0:T(8,128)(2,1)} %collective-permute-done.4, bf16[64,6144]{1,0:T(8,128)(2,1)} %collective-permute-done.3, ...), kind=kOutput, calls=%fused_computation.27 | convolution fusion | flops 306855936 | bytes 8011792 | tf_op jit(solution)/shard_map/sd,fd->sf/dot_general | solution.py:45
  186.3 63.3 %all_gather.11 = bf16[384,1024]{0,1:T(8,128)(2,1)S(1)} all-gather(bf16[384,64]{0,1:T(8,128)(2,1)S(1)} %multiply_convert_fusion), channel_id=1, replica_groups=mesh['tok'=32,'exp'=16] {'exp'}, dimensions={1}, use_global_device_ids=true | all-gather | bytes 835584 | tf_op jit(solution)/shard_map/all_gather | solution.py:47
  249.7 3.5 %convolution_convert_fusion = bf16[384,384]{1,0:T(8,128)(2,1)S(1)} fusion(bf16[384,1024]{0,1:T(8,128)(2,1)S(1)} %all_gather.11, bf16[1024,384]{1,0:T(8,128)(2,1)S(1)} %collective-permute-done.8, bf16[1024,384]{1,0:T(8,128)(2,1)S(1)} %collective-permute-done.7, bf16[1024,384]{1,0:T(8,128)(2,1)S(1)} %collective-permute-done.6, ...), kind=kOutput, calls=%fused_computation.3 | convolution fusion | flops 306855936 | bytes 4227088 | tf_op jit(solution)/shard_map/dot_general | solution.py:48
  253.2 0.1 stack_reshape.9
  253.3 0.2 pad_maximum_fusion
  253.5 1.4 copy.28
  254.9 14.9 %all-to-all-start.1 = ((bf16[2,32,12,384]{3,0,2,1:T(2,128)(2,1)}), bf16[2,32,12,384]{3,0,2,1:T(2,128)(2,1)S(1)}, u32[]{:S(2)}, u32[]{:S(2)}) async-start(bf16[2,32,12,384]{3,0,2,1:T(2,128)(2,1)} %copy.28), calls=%async_computation.1 | async-start | bytes 1179648 | tf_op jit(solution)/shard_map/all_to_all | solution.py:81
  269.9 0.1 copy.30
  270.0 15.5 %all-to-all-done.1 = bf16[2,32,12,384]{3,0,2,1:T(2,128)(2,1)S(1)} async-done(((bf16[2,32,12,384]{3,0,2,1:T(2,128)(2,1)}), bf16[2,32,12,384]{3,0,2,1:T(2,128)(2,1)S(1)}, u32[]{:S(2)}, u32[]{:S(2)}) %all-to-all-start.1) | async-done | bytes 589856 | tf_op jit(solution)/shard_map/all_to_all | solution.py:81
  285.5 0.5 convert_reduce_fusion
  286.0 0.3 fusion.2
  286.3 0.6 slice_bitcast_fusion
  (34 shorter events, 0.2 us)
Async XLA Ops:
  7.2 2.3 copy-start
  7.2 27.4 %copy-start.2 = (bf16[64,6144]{1,0:T(8,128)(2,1)S(1)}, bf16[64,6144]{1,0:T(8,128)(2,1)}, u32[]{:S(2)}) copy-start(bf16[64,6144]{1,0:T(8,128)(2,1)} %param.13) | copy-start | bytes 2359300
  7.2 38.4 %copy-start.3 = (bf16[64,6144]{1,0:T(8,128)(2,1)S(1)}, bf16[64,6144]{1,0:T(8,128)(2,1)}, u32[]{:S(2)}) copy-start(bf16[64,6144]{1,0:T(8,128)(2,1)} %param.14) | copy-start | bytes 2359300
  7.2 45.8 %copy-start.5 = (s32[4]{0:T(128)S(1)}, s32[4]{0:T(128)}, u32[]{:S(2)}) copy-start(s32[4]{0:T(128)} %param.11) | copy-start | bytes 52
  7.2 46.5 %copy-start.4 = (s32[4]{0:T(128)S(1)}, s32[4]{0:T(128)}, u32[]{:S(2)}) copy-start(s32[4]{0:T(128)} %param.12) | copy-start | bytes 52
  7.2 75.3 %all-gather.2.cloned.1.call-start = ((), (), s32[]{:S(2)}) async-start(), calls=%async_computation.2 | async-start | bytes 5013504 | tf_op jit(solution)/shard_map/all_gather | solution.py:41
  34.6 71.8 %collective-permute-start = (bf16[64,6144]{1,0:T(8,128)(2,1)S(1)}, bf16[64,6144]{1,0:T(8,128)(2,1)}, u32[]{:S(2)}, u32[]{:S(2)}) collective-permute-start(bf16[64,6144]{1,0:T(8,128)(2,1)S(1)} %copy-done.2), channel_id=1, source_target_pairs={{0,128},{16,144},{32,160},{48,176},{64,192},{80,208},{96,224},{112... | collective-permute-start | bytes 2359304 | tf_op jit(solution)/shard_map/ppermute | solution.py:13
  38.3 103.9 %collective-permute-start.2 = (bf16[64,6144]{1,0:T(8,128)(2,1)S(1)}, bf16[64,6144]{1,0:T(8,128)(2,1)}, u32[]{:S(2)}, u32[]{:S(2)}) collective-permute-start(bf16[64,6144]{1,0:T(8,128)(2,1)S(1)} %copy-done.2), channel_id=1, source_target_pairs={{0,384},{16,400},{32,416},{48,432},{64,448},{80,464},{96,480},{112... | collective-permute-start | bytes 2359304 | tf_op jit(solution)/shard_map/ppermute | solution.py:13
  42.0 104.3 %collective-permute-start.1 = (bf16[64,6144]{1,0:T(8,128)(2,1)S(1)}, bf16[64,6144]{1,0:T(8,128)(2,1)}, u32[]{:S(2)}, u32[]{:S(2)}) collective-permute-start(bf16[64,6144]{1,0:T(8,128)(2,1)S(1)} %copy-done.2), channel_id=1, source_target_pairs={{0,256},{16,272},{32,288},{48,304},{64,320},{80,336},{96,352},{112... | collective-permute-start | bytes 2359304 | tf_op jit(solution)/shard_map/ppermute | solution.py:13
  45.5 111.7 %collective-permute-start.3 = (bf16[64,6144]{1,0:T(8,128)(2,1)S(1)}, bf16[64,6144]{1,0:T(8,128)(2,1)}, u32[]{:S(2)}, u32[]{:S(2)}) collective-permute-start(bf16[64,6144]{1,0:T(8,128)(2,1)S(1)} %copy-done.3), channel_id=1, source_target_pairs={{0,128},{16,144},{32,160},{48,176},{64,192},{80,208},{96,224},{112... | collective-permute-start | bytes 2359304 | tf_op jit(solution)/shard_map/ppermute | solution.py:13
  48.5 131.9 %collective-permute-start.5 = (bf16[64,6144]{1,0:T(8,128)(2,1)S(1)}, bf16[64,6144]{1,0:T(8,128)(2,1)}, u32[]{:S(2)}, u32[]{:S(2)}) collective-permute-start(bf16[64,6144]{1,0:T(8,128)(2,1)S(1)} %copy-done.3), channel_id=1, source_target_pairs={{0,384},{16,400},{32,416},{48,432},{64,448},{80,464},{96,480},{112... | collective-permute-start | bytes 2359304 | tf_op jit(solution)/shard_map/ppermute | solution.py:13
  82.5 4.1 %copy-start.1 = (bf16[384,6144]{1,0:T(8,128)(2,1)S(1)}, bf16[384,6144]{1,0:T(8,128)(2,1)}, u32[]{:S(2)}) copy-start(bf16[384,6144]{1,0:T(8,128)(2,1)} %all-gather.2.cloned.1.call-done) | copy-start | bytes 14155780
  86.6 26.8 %copy-start.7 = (bf16[1024,384]{1,0:T(8,128)(2,1)S(1)}, bf16[1024,384]{1,0:T(8,128)(2,1)}, u32[]{:S(2)}) copy-start(bf16[1024,384]{1,0:T(8,128)(2,1)} %param.15) | copy-start | bytes 2359300
  106.4 74.0 %collective-permute-start.4 = (bf16[64,6144]{1,0:T(8,128)(2,1)S(1)}, bf16[64,6144]{1,0:T(8,128)(2,1)}, u32[]{:S(2)}, u32[]{:S(2)}) collective-permute-start(bf16[64,6144]{1,0:T(8,128)(2,1)S(1)} %copy-done.3), channel_id=1, source_target_pairs={{0,256},{16,272},{32,288},{48,304},{64,320},{80,336},{96,352},{112... | collective-permute-start | bytes 2359304 | tf_op jit(solution)/shard_map/ppermute | solution.py:13
  114.0 66.4 %slice-start = ((s8[4718592]{0:T(1024)(128)(4,1)}), s8[524288]{0:T(1024)(128)(4,1)S(1)}, s32[]{:S(2)}) async-start(s8[4718592]{0:T(1024)(128)(4,1)} %bitcast.32), calls=%async_computation.3 | async-start | bytes 1048576
  142.1 107.5 %collective-permute-start.6 = (bf16[1024,384]{1,0:T(8,128)(2,1)}, bf16[1024,384]{1,0:T(8,128)(2,1)S(1)}, u32[]{:S(2)}, u32[]{:S(2)}) collective-permute-start(bf16[1024,384]{1,0:T(8,128)(2,1)} %param.15), channel_id=1, source_target_pairs={{0,128},{16,144},{32,160},{48,176},{64,192},{80,208},{96,224},{112... | collective-permute-start | bytes 2359304 | tf_op jit(solution)/shard_map/ppermute | solution.py:13
  146.3 103.4 %collective-permute-start.8 = (bf16[1024,384]{1,0:T(8,128)(2,1)}, bf16[1024,384]{1,0:T(8,128)(2,1)S(1)}, u32[]{:S(2)}, u32[]{:S(2)}) collective-permute-start(bf16[1024,384]{1,0:T(8,128)(2,1)} %param.15), channel_id=1, source_target_pairs={{0,384},{16,400},{32,416},{48,432},{64,448},{80,464},{96,480},{112... | collective-permute-start | bytes 2359304 | tf_op jit(solution)/shard_map/ppermute | solution.py:13
  149.6 7.7 %copy-start.8 = (bf16[1024,384]{1,0:T(8,128)(2,1)S(1)}, bf16[1024,384]{1,0:T(8,128)(2,1)}, u32[]{:S(2)}) copy-start(bf16[1024,384]{1,0:T(8,128)(2,1)} %param.15) | copy-start | bytes 2359300
  149.6 30.9 %slice-start.1 = ((s8[4718592]{0:T(1024)(128)(4,1)}), s8[4194304]{0:T(1024)(128)(4,1)S(1)}, s32[]{:S(2)}) async-start(s8[4718592]{0:T(1024)(128)(4,1)} %bitcast.32), calls=%async_computation.4 | async-start | bytes 8388608
  157.3 92.4 %collective-permute-start.7 = (bf16[1024,384]{1,0:T(8,128)(2,1)S(1)}, bf16[1024,384]{1,0:T(8,128)(2,1)S(1)}, u32[]{:S(2)}, u32[]{:S(2)}) collective-permute-start(bf16[1024,384]{1,0:T(8,128)(2,1)S(1)} %copy-done.8), channel_id=1, source_target_pairs={{0,256},{16,272},{32,288},{48,304},{64,320},{80,336},{96,352},{112... | collective-permute-start | bytes 2359304 | tf_op jit(solution)/shard_map/ppermute | solution.py:13
  253.4 16.4 %copy-start.6 = (s32[16,2]{0,1:T(2,128)S(1)}, s32[16,2]{0,1:T(2,128)}, u32[]{:S(2)}) copy-start(s32[16,2]{0,1:T(2,128)} %param.10) | copy-start | bytes 388
  254.9 30.6 %all-to-all-start.1 = ((bf16[2,32,12,384]{3,0,2,1:T(2,128)(2,1)}), bf16[2,32,12,384]{3,0,2,1:T(2,128)(2,1)S(1)}, u32[]{:S(2)}, u32[]{:S(2)}) async-start(bf16[2,32,12,384]{3,0,2,1:T(2,128)(2,1)} %copy.28), calls=%async_computation.1 | async-start | bytes 1179648 | tf_op jit(solution)/shard_map/all_to_all | solution.py:81
Sparse Core Ops, SparseCore 0:
  34.7 47.7 all-gather.1
where the time goes:
time: 297 us; the launch traced here: 294 us
  blocking collectives  106 us (36%)
  waiting for transfers between devices  86.6 us (29%)
  starting transfers between devices  53.3 us (18%)
  matrix products  23.7 us (8%)
  between operations  14.5 us (5%)
  other arithmetic  5.72 us (2%)
  local copies, waits for them, and re-layouts  4.15 us (1%)
    all_gather x2, blocking collectives, project(): units = lax.all_gather(hidden, 'exp', axis=1, tiled=True)  81.5 us
    ppermute x9, waiting for transfers between devices, passed_along(): lax.ppermute(value, axis, [(i, (i + by) % devices) for i in range(devices)])  45.5 us
    ppermute x9, starting transfers between devices, passed_along(): lax.ppermute(value, axis, [(i, (i + by) % devices) for i in range(devices)])  38.4 us
    all_gather x1, waiting for transfers between devices, local(): rows = lax.all_gather(rows_part, 'exp', axis=1, tiled=True)  25.6 us
    all_to_all x1, blocking collectives, local(): lax.all_to_all(copies, 'tok', split_axis=0, concat_axis=0, tiled=True)  24.1 us
    all_to_all x1, waiting for transfers between devices, local(): lax.all_to_all(stacked.astype(jnp.bfloat16), 'tok', split_axis=1, concat_...  15.5 us
    all_to_all x1, starting transfers between devices, local(): lax.all_to_all(stacked.astype(jnp.bfloat16), 'tok', split_axis=1, concat_...  14.9 us
    dot_general x2, matrix products, project(): jnp.einsum('sd,fd->sf', rows, gate_w, preferred_element_type=jnp.float32)  11.7 us
  transfers between devices with their start and end apart: 11, of which 4 were waited for; matrix products, arithmetic and copies ran while one was open for 8% of the time, Pallas kernels for 0%

commit v1 on v0

v1 whole, which is shorter than its diff:
```python
import jax
import jax.numpy as jnp
from jax import lax
from jax.sharding import PartitionSpec as P

EXPERTS = 4
LANES = 128


def local(tokens, route_ids, gate_codes, merge_labels, freq_counts, w_gate, w_up, w_down):
    n_tok = lax.axis_size("tok")
    span = n_tok // EXPERTS
    expert = lax.axis_index("tok") // span
    tok_dev, width = tokens.shape
    units = w_gate.shape[0]
    ids = jnp.arange(LANES, dtype=jnp.int32)
    scale = gate_codes.astype(jnp.float32) / 256.0
    share = jnp.sum(jnp.where(route_ids[:, :, None] == ids, scale[:, :, None], 0.0), axis=1)
    wide = lax.all_gather(tokens, "exp", axis=1, tiled=True)
    wide = jnp.concatenate([wide, share.astype(jnp.bfloat16)], axis=1)
    every = lax.all_gather(wide, "tok", axis=0, tiled=True)
    depth = every.shape[1] - LANES
    rows, share = every[:, :depth], every[:, depth : depth + EXPERTS].astype(jnp.float32)

    freq = freq_counts.astype(jnp.float32)
    experts = jnp.arange(EXPERTS, dtype=jnp.int32)
    own_label = jnp.sum(jnp.where(experts == expert, merge_labels, 0))
    member = merge_labels == own_label
    total = jnp.sum(jnp.where(member, freq, 0.0))
    own = jnp.sum(jnp.where(experts == expert, freq, 0.0)) / total
    other = jnp.sum(jnp.where(member & (experts != expert), freq, 0.0)) / total

    both = jnp.concatenate([w_gate, w_up], axis=0)
    first = jnp.einsum("nd,fd->nf", rows, both, preferred_element_type=jnp.float32)
    partner = jnp.where(
        merge_labels[1] == merge_labels[0], 0, jnp.where(merge_labels[2] == merge_labels[0], 1, 2)
    )

    def swap(mask):
        def run(value):
            pairs = [(i, (((i // span) ^ mask) * span) + i % span) for i in range(n_tok)]
            return lax.ppermute(value, "tok", pairs)

        return run

    sent = first.astype(jnp.bfloat16)
    got = lax.switch(partner, [swap(1), swap(2), swap(3)], sent)
    merged = own * first + other * got.astype(jnp.float32)

    def act(v):
        return (jax.nn.silu(v[:, :units]) * v[:, units:]).astype(jnp.bfloat16)

    hidden = jnp.concatenate([act(first), act(merged)], axis=0)
    hidden = lax.all_gather(hidden, "exp", axis=1, tiled=True)
    out = jnp.dot(hidden, w_down, preferred_element_type=jnp.float32)
    take_own = jnp.sum(jnp.where(experts == expert, share, 0.0), axis=1)
    take_group = own * jnp.sum(jnp.where(member, share, 0.0), axis=1)
    weight = jnp.concatenate([take_own, take_group])
    out = (out * weight[:, None]).astype(jnp.bfloat16)
    out = out.reshape(2, n_tok, tok_dev, width)
    out = lax.all_to_all(out, "tok", split_axis=1, concat_axis=1, tiled=True)
    out = jnp.sum(out.astype(jnp.float32), axis=1).astype(jnp.bfloat16)
    return out[0], out[1]


def solution(mesh):
    return jax.shard_map(
        local,
        mesh=mesh,
        in_specs=(
            P("tok", "exp"),
            P("tok", None),
            P("tok", None),
            P(),
            P(),
            P(("tok", "exp"), None),
            P(("tok", "exp"), None),
            P("tok", "exp"),
        ),
        out_specs=(P("tok", "exp"), P("tok", "exp")),
        check_vma=False,
    )
```

time: 297 us -> 228 us (0.77)
  starting transfers between devices: 53.3 us -> 2.99 us
  blocking collectives: 106 us -> 55.7 us
  waiting for transfers between devices: 86.6 us -> 128 us
  matrix products: 23.7 us -> 8.27 us
  between operations: 14.5 us -> 19.3 us
    all_gather x1 -> x2, waiting for transfers between devices: 25.6 us -> 120 us  [the longest x1 79.9 us: local(): every = lax.all_gather(wide, 'tok', axis=0, tiled=True)]
    all_gather x2 -> x1, blocking collectives: 81.5 us -> 25.2 us  [local(): wide = lax.all_gather(tokens, 'exp', axis=1, tiled=True)]
    ppermute x9 -> x1, waiting for transfers between devices: 45.5 us -> 7.65 us  [run(): return lax.ppermute(value, 'tok', pairs)]
    ppermute x9 -> x1, starting transfers between devices: 38.4 us -> 2.91 us  [run(): return lax.ppermute(value, 'tok', pairs)]
    all_to_all x1 -> x0, waiting for transfers between devices: 15.5 us -> none  [local(): lax.all_to_all(stacked.astype(jnp.bfloat16), 'tok', split_axis=1, concat_...]
    dot_general x8 -> x2, matrix products: 23.7 us -> 8.27 us  [the longest x1 5.4 us: local(): jnp.einsum('nd,fd->nf', rows, both, preferred_element_type=jnp.float32)]
    all_to_all x1 -> x0, starting transfers between devices: 14.9 us -> none  [local(): lax.all_to_all(stacked.astype(jnp.bfloat16), 'tok', split_axis=1, concat_...]
    all_to_all x1, blocking collectives: 24.1 us -> 30.4 us  [local(): out = lax.all_to_all(out, 'tok', split_axis=1, concat_axis=1, tiled=True)]
  transfers between devices with their start and end apart: 11 -> 3, of which waited for: 4 -> 3; matrix products, arithmetic and copies ran while one was open for 8% -> 3% of each run, Pallas kernels for 0% -> 0%
where the time goes in v1:
time: 228 us; the launch traced here: 225 us
  waiting for transfers between devices  128 us (56%)
  blocking collectives  55.7 us (24%)
  between operations  19.3 us (8%)
  matrix products  8.27 us (4%)
  other arithmetic  7.41 us (3%)
  local copies, waits for them, and re-layouts  3.21 us (1%)
  starting transfers between devices  2.99 us (1%)
    all_gather x1, waiting for transfers between devices, local(): every = lax.all_gather(wide, 'tok', axis=0, tiled=True)  79.9 us
    all_gather x1, waiting for transfers between devices, local(): hidden = lax.all_gather(hidden, 'exp', axis=1, tiled=True)  40.6 us
    all_to_all x1, blocking collectives, local(): out = lax.all_to_all(out, 'tok', split_axis=1, concat_axis=1, tiled=True)  30.4 us
    all_gather x1, blocking collectives, local(): wide = lax.all_gather(tokens, 'exp', axis=1, tiled=True)  25.2 us
    ppermute x1, waiting for transfers between devices, run(): return lax.ppermute(value, 'tok', pairs)  7.65 us
    dot_general x1, matrix products, local(): jnp.einsum('nd,fd->nf', rows, both, preferred_element_type=jnp.float32)  5.4 us
  transfers between devices with their start and end apart: 3, of which 3 were waited for; matrix products, arithmetic and copies ran while one was open for 3% of the time, Pallas kernels for 0%

profile of v1, /device:TPU:1, one launch (start us, length us, event | category | flops | bytes accessed | tf_op | source)
XLA Modules:
  0.0 225.0 jit_solution(12899594071152001083)
XLA Ops:
  7.2 0.0 copy-start
  7.2 0.0 all-gather.3.cloned.1.call-start
  7.2 0.7 convert_multiply_fusion
  8.0 25.2 %all_gather.9 = bf16[16,6144]{1,0:T(8,128)(2,1)S(1)} all-gather(bf16[16,384]{1,0:T(8,128)(2,1)} %param.11), channel_id=1, replica_groups=mesh['tok'=32,'exp'=16] {'exp'}, dimensions={1}, use_global_device_ids=true | all-gather | bytes 208896 | tf_op jit(solution)/shard_map/all_gather | solution.py:19
  33.2 0.8 select_reduce_fusion
  34.0 0.7 pad_maximum_fusion
  34.7 0.0 all-gather.3.cloned.1.call-update
  34.7 0.0 all-gather.5.cloned.1.call-start
  34.7 1.3 select_reduce_fusion.2
  36.0 2.0 select_reduce_fusion.1
  40.6 1.4 fusion.11
  44.5 79.9 %all-gather.3.cloned.1.call-done = bf16[512,6272]{1,0:T(8,128)(2,1)} async-done(((bf16[16,6272]{1,0:T(8,128)(2,1)}), bf16[512,6272]{1,0:T(8,128)(2,1)}) %all-gather.3.cloned.1.call-update) | async-done | bytes 6422544 | tf_op jit(solution)/shard_map/all_gather | solution.py:21
  124.4 5.4 %fusion.12 = (bf16[512,128]{0,1:T(8,128)(2,1)S(1)}, f32[512,128]{0,1:T(8,128)S(1)}) fusion(bf16[64,6144]{1,0:T(8,128)(2,1)} %param.17, bf16[64,6144]{1,0:T(8,128)(2,1)} %param.16, bf16[512,6272]{1,0:T(8,128)(2,1)} %all-gather.3.cloned.1.call-done), kind=kOutput, calls=%fused_computation.33 | convolution fusion | flops 808517632 | bytes 8257536 | tf_op jit(solution)/shard_map/nd,fd->nf/dot_general | solution.py:34
  129.8 10.7 %conditional.4 = (bf16[512,128]{1,0:T(8,128)(2,1)}) conditional(s32[]{:T(128)} %bitcast, bf16[512,128]{0,1:T(8,128)(2,1)S(1)} %get-tuple-element.26, bf16[512,128]{0,1:T(8,128)(2,1)S(1)} %get-tuple-element.26, bf16[512,128]{0,1:T(8,128)(2,1)S(1)} %get-tuple-element.26), branch_computations={%region_5.6_spmd, %region_6.7_spmd, %region_7.8_spmd} | conditional | bytes 786480
  129.8 0.1 copy.23
  129.9 2.9 %collective-permute-start = (bf16[512,128]{1,0:T(8,128)(2,1)S(1)}, bf16[512,128]{1,0:T(8,128)(2,1)}, u32[]{:S(2)}, u32[]{:S(2)}) collective-permute-start(bf16[512,128]{1,0:T(8,128)(2,1)S(1)} %copy.23), channel_id=1, source_target_pairs={{0,128},{16,144},{32,160},{48,176},{64,192},{80,208},{96,224},{112... | collective-permute-start | bytes 393224 | tf_op jit(solution)/shard_map/cond/branch_0_fun/ppermute | solution.py:42
  132.9 7.6 %collective-permute-done = bf16[512,128]{1,0:T(8,128)(2,1)} collective-permute-done((bf16[512,128]{1,0:T(8,128)(2,1)S(1)}, bf16[512,128]{1,0:T(8,128)(2,1)}, u32[]{:S(2)}, u32[]{:S(2)}) %collective-permute-start) | collective-permute-done | bytes 131104 | tf_op jit(solution)/shard_map/cond/branch_0_fun/ppermute | solution.py:42
  140.5 1.0 copy.26
  141.6 0.1 fusion.7
  141.7 0.6 pad_maximum_fusion.1
  142.3 0.0 all-gather.5.cloned.1.call-update
  142.3 1.1 fusion.5
  143.4 40.6 %all-gather.5.cloned.1.call-done = bf16[1024,1024]{0,1:T(8,128)(2,1)} async-done(((bf16[1024,64]{0,1:T(8,128)(2,1)}), bf16[1024,1024]{0,1:T(8,128)(2,1)}) %all-gather.5.cloned.1.call-update) | async-done | bytes 2097168 | tf_op jit(solution)/shard_map/all_gather | solution.py:54
  184.0 0.0 copy-done
  184.0 2.9 %multiply_convert_fusion = bf16[1024,384]{1,0:T(8,128)(2,1)S(1)} fusion(bf16[1024,1024]{0,1:T(8,128)(2,1)} %all-gather.5.cloned.1.call-done, bf16[1024,384]{1,0:T(8,128)(2,1)S(1)} %copy-done, f32[1024]{0:T(1024)S(1)} %pad_maximum_fusion.2), kind=kOutput, calls=%fused_computation.5 | convolution fusion | flops 806092800 | bytes 3674112 | tf_op jit(solution)/shard_map/dot_general | solution.py:55
  186.9 0.1 copy.27
  187.0 30.4 %all_to_all.5 = bf16[2,32,16,384]{3,2,0,1:T(8,128)(2,1)S(1)} all-to-all(bf16[2,32,16,384]{3,2,0,1:T(8,128)(2,1)S(1)} %copy.27), channel_id=1, replica_groups=mesh['tok'=32,'exp'=16] {'tok'}, dimensions={1} | all-to-all | bytes 1572864 | tf_op jit(solution)/shard_map/all_to_all | solution.py:61
  217.4 0.1 reduce_sum.82
  217.5 0.6 slice_bitcast_fusion
  (4 shorter events, 0.1 us)
Async XLA Ops:
  7.2 176.8 %copy-start = (bf16[1024,384]{1,0:T(8,128)(2,1)S(1)}, bf16[1024,384]{1,0:T(8,128)(2,1)}, u32[]{:S(2)}) copy-start(bf16[1024,384]{1,0:T(8,128)(2,1)} %param.18) | copy-start | bytes 2359300
  7.2 117.2 %all-gather.3.cloned.1.call-start = ((), (), s32[]{:S(2)}) async-start(), calls=%async_computation.1 | async-start | bytes 6623232 | tf_op jit(solution)/shard_map/all_gather | solution.py:21
  34.7 149.3 %all-gather.5.cloned.1.call-start = ((), (), s32[]{:S(2)}) async-start(), calls=%async_computation.2 | async-start | bytes 2228224 | tf_op jit(solution)/shard_map/all_gather | solution.py:54
  129.9 10.6 %collective-permute-start = (bf16[512,128]{1,0:T(8,128)(2,1)S(1)}, bf16[512,128]{1,0:T(8,128)(2,1)}, u32[]{:S(2)}, u32[]{:S(2)}) collective-permute-start(bf16[512,128]{1,0:T(8,128)(2,1)S(1)} %copy.23), channel_id=1, source_target_pairs={{0,128},{16,144},{32,160},{48,176},{64,192},{80,208},{96,224},{112... | collective-permute-start | bytes 393224 | tf_op jit(solution)/shard_map/cond/branch_0_fun/ppermute | solution.py:42
Sparse Core Ops, SparseCore 0:
  34.8 89.5 all-gather.2
  142.4 41.5 all-gather.4

commit v2 on v1

v2 whole, which is shorter than its diff:
```python
import functools

import jax
import jax.numpy as jnp
from jax import lax
from jax.experimental import pallas as pl
from jax.experimental.pallas import tpu as pltpu
from jax.sharding import PartitionSpec as P

EXPERTS = 4
LANES = 128
NX, NY, NZ = 4, 8, 8
MESH = pl.DeviceIdType.MESH
BF16, F32 = jnp.bfloat16, jnp.float32
ORDER = (0, -1, 1, -2, 2, -3, 3, -4)
UP_STEPS, DOWN_STEPS = 4, 3


def kernel(
    flip, labels, freq, tokens, share, w_gate, w_up, w_down, first_out, second_out,
    rows, wcat, wd, part, part_in, full, swap, swap_in, hid, ysend, yrecv, yown, xsend, xrecv, fsend, frecv,
    t_loc, w_loc, w_snd, w_rcv, z_snd, z_rcv, up_snd, up_rcv, dn_snd, dn_rcv,
    xr_snd, xr_rcv, xl_snd, xl_rcv, fr_snd, fr_rcv, fl_snd, fl_rcv,
    p_snd, p_rcv, e_snd, e_rcv, h_snd, h_rcv, y_snd, y_rcv, x_snd, x_rcv, f_snd, f_rcv,
):
    tok, exp = lax.axis_index("tok"), lax.axis_index("exp")
    y, x = tok // NX, tok % NX
    z, core = exp // 2, exp % 2
    sib = (tok, z * 2 + (1 - core))
    half = w_gate.shape[0]
    units = 2 * half
    tok_dev, width = tokens.shape
    planes = width // LANES
    total = NZ * planes + 1
    span = NX * tok_dev
    expert = y // 2

    def at_z(k):
        return (tok, ((z + k) % NZ) * 2 + core)

    def at_y(k):
        return (((y + k) % NY) * NX + x, exp)

    def at_x(k):
        return (y * NX + (x + k) % NX, exp)

    def remote(src, dst, snd, rcv, dev):
        return pltpu.make_async_remote_copy(
            src_ref=src, dst_ref=dst, send_sem=snd, recv_sem=rcv, device_id=dev, device_id_type=MESH
        )

    def rows_of(t, lo=0, n=None):
        n = total if n is None else n
        return rows.at[pl.ds(lo, n), pl.ds(pl.multiple_of(t * tok_dev, tok_dev), tok_dev), :]

    mine = pl.ds(pl.multiple_of(tok * tok_dev, tok_dev), tok_dev)
    locals_ = []
    for i in range(planes):
        locals_.append(
            pltpu.make_async_copy(
                tokens.at[:, pl.ds(i * LANES, LANES)], rows.at[z * planes + i, mine, :], t_loc.at[i]
            )
        )
    locals_.append(pltpu.make_async_copy(share, rows.at[NZ * planes, mine, :], t_loc.at[planes]))
    for copy in locals_:
        copy.start()

    barrier = pltpu.get_barrier_semaphore()
    greeted = [at_z(k) for k in range(1, NZ)] + [at_y(k) for k in range(1, NY)]
    greeted += [at_x(k) for k in range(1, NX)] + [sib]
    for dev in greeted:
        pl.semaphore_signal(barrier, inc=1, device_id=dev, device_id_type=MESH)

    loads = []
    for zz in range(NZ):
        for which, ref in enumerate((w_gate, w_up)):
            dst = wcat.at[zz, pl.ds(pl.multiple_of(which * units + core * half, half), half), :]
            cols = pl.ds(pl.multiple_of((2 * zz + core) * width, LANES), width)
            loads.append(pltpu.make_async_copy(ref.at[:, cols], dst, w_loc.at[2 * zz + which]))
    wide = pl.ds(pl.multiple_of(core * width, LANES), width)
    loads.append(pltpu.make_async_copy(w_down, wd.at[:, wide], w_loc.at[2 * NZ]))
    for copy in loads:
        copy.start()
    for copy in locals_:
        copy.wait()
    pl.semaphore_wait(barrier, len(greeted))

    zs = []
    own_planes = rows.at[pl.ds(z * planes, planes), mine, :]
    for k in (1, 7, 2, 6, 3, 5, 4):
        zs.append(remote(own_planes, own_planes, z_snd.at[k], z_rcv.at[k], at_z(k)))
    for copy in zs:
        copy.start()

    gifts = []
    for zz in range(NZ):
        for which, ref in enumerate((w_gate, w_up)):
            dst = wcat.at[zz, pl.ds(pl.multiple_of(which * units + core * half, half), half), :]
            cols = pl.ds(pl.multiple_of((2 * zz + (1 - core)) * width, LANES), width)
            i = 2 * zz + which
            gifts.append(remote(ref.at[:, cols], dst, w_snd.at[i], w_rcv.at[i], sib))
    gifts.append(remote(w_down, wd.at[:, wide], w_snd.at[2 * NZ], w_rcv.at[2 * NZ], sib))
    for copy in gifts:
        copy.start()

    for k in range(1, NZ):
        got = rows.at[pl.ds(((z - k) % NZ) * planes, planes), mine, :]
        remote(got, got, z_snd.at[k], z_rcv.at[k], at_z(k)).wait_recv()

    def group(k):
        return (y + ORDER[k]) % NY

    sent = []

    def send(*args):
        copy = remote(*args)
        copy.start()
        sent.append(copy)

    def along_y(k):
        block = rows_of(group(k) * NX + x)
        off = ORDER[k]
        if off <= 0 and -off < UP_STEPS:
            send(block, block, up_snd.at[-off], up_rcv.at[-off], at_y(1))
        if off >= 0 and off < DOWN_STEPS:
            send(block, block, dn_snd.at[off], dn_rcv.at[off], at_y(-1))

    def from_y(k):
        block = rows_of(group(k) * NX + x)
        off = ORDER[k]
        if off < 0:
            remote(block, block, up_snd.at[-off - 1], up_rcv.at[-off - 1], at_y(1)).wait_recv()
        elif off > 0:
            remote(block, block, dn_snd.at[off - 1], dn_rcv.at[off - 1], at_y(-1)).wait_recv()

    def along_x(k):
        block = rows_of(group(k) * NX + x)
        send(block, block, xr_snd.at[k], xr_rcv.at[k], at_x(1))
        send(block, block, xl_snd.at[k], xl_rcv.at[k], at_x(-1))

    low = total // 2

    def from_x(k):
        left = rows_of(group(k) * NX + (x - 1) % NX)
        remote(left, left, xr_snd.at[k], xr_rcv.at[k], at_x(1)).wait_recv()
        piece = rows_of(group(k) * NX + (x - 1) % NX, 0, low)
        send(piece, piece, fr_snd.at[k], fr_rcv.at[k], at_x(1))
        right = rows_of(group(k) * NX + (x + 1) % NX)
        remote(right, right, xl_snd.at[k], xl_rcv.at[k], at_x(-1)).wait_recv()
        piece = rows_of(group(k) * NX + (x + 1) % NX, low, total - low)
        send(piece, piece, fl_snd.at[k], fl_rcv.at[k], at_x(-1))

    def from_far(k):
        piece = rows_of(group(k) * NX + (x + 2) % NX, 0, low)
        remote(piece, piece, fr_snd.at[k], fr_rcv.at[k], at_x(1)).wait_recv()
        piece = rows_of(group(k) * NX + (x + 2) % NX, low, total - low)
        remote(piece, piece, fl_snd.at[k], fl_rcv.at[k], at_x(-1)).wait_recv()

    def span_of(k):
        return pl.ds(pl.multiple_of(group(k) * span, span), span)

    nt = (((1,), (1,)), ((), ()))

    def multiply(k):
        here = span_of(k)
        acc = jnp.zeros((span, 2 * units), F32)
        for j in range(NZ * planes // 2):
            a, b = 2 * j, 2 * j + 1
            lhs = jnp.concatenate([rows[a, here, :], rows[b, here, :]], axis=1)
            rhs = jnp.concatenate(
                [
                    wcat[a // planes, :, (a % planes) * LANES : (a % planes + 1) * LANES],
                    wcat[b // planes, :, (b % planes) * LANES : (b % planes + 1) * LANES],
                ],
                axis=1,
            )
            acc = acc + lax.dot_general(lhs, rhs, nt, preferred_element_type=F32)
        part[here, :] = acc
        send(part.at[here, :], part_in.at[here, :], p_snd.at[k], p_rcv.at[k], sib)

    partner_tok = (((expert ^ flip) * 2 + (y % 2)) * NX) + x

    def joined(k):
        here = span_of(k)
        remote(part.at[here, :], part_in.at[here, :], p_snd.at[k], p_rcv.at[k], sib).wait_recv()
        both = part[here, :] + part_in[here, :]
        full[here, :] = both
        swap[here, :] = both.astype(BF16)

    def swap_copy(k):
        here = span_of(k)
        g = group(k)
        return remote(swap.at[here, :], swap_in.at[here, :], e_snd.at[g], e_rcv.at[g], (partner_tok, exp))

    def to_partner(k):
        @pl.when(core == 1)
        def _():
            swap_copy(k).start()

    lane = lax.broadcasted_iota(jnp.int32, (1, LANES), 1)
    zero = jnp.zeros((1, LANES), F32)
    freq_v, label_v = zero, jnp.full((1, LANES), -1, jnp.int32)
    own_label = jnp.int32(0)
    for e in range(EXPERTS):
        freq_v = jnp.where(lane == e, freq[e].astype(F32), freq_v)
        label_v = jnp.where(lane == e, labels[e], label_v)
        own_label = jnp.where(expert == e, labels[e], own_label)
    member = jnp.where(label_v == own_label, 1.0, 0.0).astype(F32)
    member_freq = member * freq_v
    coef = member_freq / jnp.sum(member_freq, axis=1, keepdims=True)
    own_lane = jnp.where(lane == expert, 1.0, 0.0).astype(F32)
    own = jnp.sum(coef * own_lane, axis=1, keepdims=True)
    other = jnp.sum(coef * (1.0 - own_lane), axis=1, keepdims=True)
    taken = jnp.where(core == 1, own * member, own_lane)

    def activate(k):
        here = span_of(k)

        @pl.when(core == 1)
        def _():
            swap_copy(k).wait_recv()
            v = own * full[here, :] + other * swap_in[here, :].astype(F32)
            full[here, :] = v

        v = full[here, :]
        gate, upper = v[:, :units], v[:, units:]
        hid[z, here, :] = (gate / (1.0 + jnp.exp(-gate)) * upper).astype(BF16)

    def along_z(k):
        here = span_of(k)
        for d in (4, 3, 5, 2, 6, 1, 7):
            remote(hid.at[z, here, :], hid.at[z, here, :], h_snd.at[k], h_rcv.at[k], at_z(d)).start()

    def finish(k):
        here = span_of(k)
        seven = hid.at[pl.ds(0, NZ - 1), here, :]
        pltpu.make_async_copy(seven, seven, h_rcv.at[k]).wait()
        acc = jnp.zeros((span, 2 * width), F32)
        for j in range(NZ // 2):
            lhs = jnp.concatenate([hid[2 * j, here, :], hid[2 * j + 1, here, :]], axis=1)
            acc = acc + jnp.dot(
                lhs, wd[2 * j * units : 2 * (j + 1) * units, :], preferred_element_type=F32
            )
        weight = jnp.sum(rows[NZ * planes, here, :].astype(F32) * taken, axis=1, keepdims=True)
        acc = acc * weight
        if k == 0:
            yown[...] = acc
        else:
            ysend[k] = acc.astype(BF16)
            send(ysend.at[k], yrecv.at[k], y_snd.at[k], y_rcv.at[k], at_y(ORDER[k]))

    along_y(0)
    along_x(0)
    for copy in loads:
        copy.wait()
    for k in range(NY):
        if k + 1 < NY:
            from_y(k + 1)
            along_y(k + 1)
            along_x(k + 1)
        from_x(k)
        if k == 1:
            for zz in range(NZ):
                for which in range(2):
                    i = 2 * zz + which
                    dst = wcat.at[zz, pl.ds(pl.multiple_of(which * units + (1 - core) * half, half), half), :]
                    remote(dst, dst, w_snd.at[i], w_rcv.at[i], sib).wait_recv()
        if k >= 1:
            from_far(k - 1)
            multiply(k - 1)
        if k >= 2:
            joined(k - 2)
            if k >= 3:
                to_partner(k - 3)
    from_far(NY - 1)
    multiply(NY - 1)
    joined(NY - 2)
    to_partner(NY - 3)
    joined(NY - 1)
    to_partner(NY - 2)
    theirs = wd.at[:, pl.ds(pl.multiple_of((1 - core) * width, LANES), width)]
    remote(theirs, theirs, w_snd.at[2 * NZ], w_rcv.at[2 * NZ], sib).wait_recv()
    to_partner(NY - 1)
    for k in range(NY):
        activate(k)
        if k >= 1:
            along_z(k - 1)
        if k >= 3:
            finish(k - 3)
    along_z(NY - 1)
    for k in range(NY - 3, NY):
        finish(k)

    acc = yown[...]
    for k in range(1, NY):
        remote(ysend.at[k], yrecv.at[k], y_snd.at[k], y_rcv.at[k], at_y(ORDER[k])).wait_recv()
        acc = acc + yrecv[k].astype(F32)
    xsend[...] = acc.astype(BF16).reshape(NX, tok_dev, 2 * width)
    yown[...] = acc
    for k in range(1, NX):
        send(xsend.at[(x + k) % NX], xrecv.at[k], x_snd.at[k], x_rcv.at[k], at_x(k))
    acc = yown[pl.ds(pl.multiple_of(x * tok_dev, tok_dev), tok_dev), :]
    for k in range(1, NX):
        remote(xsend.at[0], xrecv.at[k], x_snd.at[k], x_rcv.at[k], at_x(k)).wait_recv()
        acc = acc + xrecv[k].astype(F32)
    kept = jnp.where(core == 0, acc[:, :width], acc[:, width:]).astype(BF16)
    fsend[...] = jnp.where(core == 0, acc[:, width:], acc[:, :width]).astype(BF16)
    send(fsend, frecv, f_snd, f_rcv, sib)
    remote(fsend, frecv, f_snd, f_rcv, sib).wait_recv()
    back = frecv[...]
    first_out[...] = jnp.where(core == 0, kept, back)
    second_out[...] = jnp.where(core == 0, back, kept)

    for copy in zs + gifts + sent:
        copy.wait_send()
    for k in range(NY):
        seven = hid.at[pl.ds(0, NZ - 1), span_of(k), :]
        pltpu.make_async_copy(seven, seven, h_snd.at[k]).wait()

    @pl.when(core == 1)
    def _():
        for k in range(NY):
            swap_copy(k).wait_send()


def local(tokens, route_ids, gate_codes, merge_labels, freq_counts, w_gate, w_up, w_down):
    ids = jnp.arange(LANES, dtype=jnp.int32)
    scale = gate_codes.astype(F32) / 256.0
    share = jnp.sum(jnp.where(route_ids[:, :, None] == ids, scale[:, :, None], 0.0), axis=1)
    share = share.astype(BF16)
    tok_dev, width = tokens.shape
    half = w_gate.shape[0]
    count, depth = NX * NY * tok_dev, w_down.shape[0]
    units = 2 * half
    planes = width // LANES
    span = NX * tok_dev
    dma = pltpu.SemaphoreType.DMA
    scratch = [
        pltpu.VMEM((NZ * planes + 1, count, LANES), BF16),
        pltpu.VMEM((NZ, 2 * units, width), BF16),
        pltpu.VMEM((depth, 2 * width), BF16),
        pltpu.VMEM((count, 2 * units), F32),
        pltpu.VMEM((count, 2 * units), F32),
        pltpu.VMEM((count, 2 * units), F32),
        pltpu.VMEM((count, 2 * units), BF16),
        pltpu.VMEM((count, 2 * units), BF16),
        pltpu.VMEM((NZ, count, units), BF16),
        pltpu.VMEM((NY, span, 2 * width), BF16),
        pltpu.VMEM((NY, span, 2 * width), BF16),
        pltpu.VMEM((span, 2 * width), F32),
        pltpu.VMEM((NX, tok_dev, 2 * width), BF16),
        pltpu.VMEM((NX, tok_dev, 2 * width), BF16),
        pltpu.VMEM((tok_dev, width), BF16),
        pltpu.VMEM((tok_dev, width), BF16),
        dma((planes + 1,)),
        dma((2 * NZ + 1,)),
        dma((2 * NZ + 1,)),
        dma((2 * NZ + 1,)),
        dma((NZ,)),
        dma((NZ,)),
        *[dma((NY // 2,))] * 4,
        *[dma((NY,))] * 16,
        dma((NX,)),
        dma((NX,)),
        dma(()),
        dma(()),
    ]
    smem, hbm = pl.BlockSpec(memory_space=pltpu.SMEM), pl.BlockSpec(memory_space=pl.ANY)
    vmem = pl.BlockSpec(memory_space=pltpu.VMEM)
    out = jax.ShapeDtypeStruct((tok_dev, width), BF16)

    def variant(flip):
        def run(*args):
            return pl.pallas_call(
                functools.partial(kernel, flip),
                out_shape=(out, out),
                in_specs=[smem, smem, hbm, hbm, hbm, hbm, hbm],
                out_specs=(vmem, vmem),
                scratch_shapes=scratch,
                compiler_params=pltpu.CompilerParams(
                    collective_id=flip, has_side_effects=True, vmem_limit_bytes=40 * 1024 * 1024
                ),
                name=f"layer_flip{flip}",
            )(*args)

        return run

    same = merge_labels[1:] == merge_labels[0]
    pairing = jnp.where(same[0], 0, jnp.where(same[1], 1, 2))
    return lax.switch(
        pairing,
        [variant(1), variant(2), variant(3)],
        merge_labels, freq_counts, tokens, share, w_gate, w_up, w_down,
    )


def solution(mesh):
    return jax.shard_map(
        local,
        mesh=mesh,
        in_specs=(
            P("tok", "exp"),
            P("tok", None),
            P("tok", None),
            P(),
            P(),
            P(("tok", "exp"), None),
            P(("tok", "exp"), None),
            P("tok", "exp"),
        ),
        out_specs=(P("tok", "exp"), P("tok", "exp")),
        check_vma=False,
    )
```

time: 228 us -> 106 us (0.46); the launches traced: 225 us -> 107 us
  waiting for transfers between devices: 128 us -> 0 us
  Pallas kernels: 0 us -> 101 us
  blocking collectives: 55.7 us -> 0 us
  between operations: 19.3 us -> 1.97 us
  matrix products: 8.27 us -> 0 us
  other arithmetic: 7.41 us -> 0.19 us
  starting transfers between devices: 2.99 us -> 0 us
    all_gather x2 -> x0, waiting for transfers between devices: 120 us -> none  [the longest x1 79.9 us: local(): every = lax.all_gather(wide, 'tok', axis=0, tiled=True)]
    pallas_call x0 -> x1, Pallas kernels: none -> 101 us  [run(): pl.pallas_call(functools.partial(kernel, flip), out_shape=(out, out), in_...]
    all_to_all x1 -> x0, blocking collectives: 30.4 us -> none  [local(): out = lax.all_to_all(out, 'tok', split_axis=1, concat_axis=1, tiled=True)]
    all_gather x1 -> x0, blocking collectives: 25.2 us -> none  [local(): wide = lax.all_gather(tokens, 'exp', axis=1, tiled=True)]
    dot_general x2 -> x0, matrix products: 8.27 us -> none  [the longest x1 5.4 us: local(): jnp.einsum('nd,fd->nf', rows, both, preferred_element_type=jnp.float32)]
    ppermute x1 -> x0, waiting for transfers between devices: 7.65 us -> none  [run(): return lax.ppermute(value, 'tok', pairs)]
    reduce_sum x4 -> x0, other arithmetic: 4.43 us -> none  [the longest x1 1.96 us: local(): total = jnp.sum(jnp.where(member, freq, 0.0))]
    unnamed x2 -> x12, local copies, waits for them, and re-layouts: 0.01 us -> 3.78 us
  transfers between devices with their start and end apart: 3 -> 0, of which waited for: 3 -> 0; matrix products, arithmetic and copies ran while one was open for 3% -> 0% of each run, Pallas kernels for 0% -> 0%
where the time goes in v2:
time: 106 us; the launch traced here: 107 us
  Pallas kernels  101 us (95%)
  local copies, waits for them, and re-layouts  4.37 us (4%)
  between operations  1.97 us (2%)
    pallas_call x1, Pallas kernels, run(): pl.pallas_call(functools.partial(kernel, flip), out_shape=(out, out), in_...  101 us
    unnamed x12, local copies, waits for them, and re-layouts  3.78 us

profile of v2, /device:TPU:1, one launch (start us, length us, event | category | flops | bytes accessed | tf_op | source)
XLA Modules:
  0.0 107.4 jit_solution(249508565801889119)
XLA Ops:
  0.6 0.0 copy-start.1
  0.6 0.6 copy-done.1
  1.3 0.0 copy-start
  1.3 0.1 slice_compare_fusion
  1.4 0.6 fusion
  3.3 0.0 copy-start.3
  3.3 0.7 copy-done.3
  4.0 0.0 copy-start.4
  4.0 0.7 copy-done.4
  4.7 0.0 copy-start.2
  4.7 0.1 select_reduce_fusion
  4.7 0.0 copy-done
  4.7 0.6 copy-done.2
  5.3 100.9 %conditional.1 = ((bf16[16,384]{1,0:T(8,128)(2,1)S(1)}, bf16[16,384]{1,0:T(8,128)(2,1)S(1)})) conditional(s32[]{:T(128)} %bitcast.1, (s32[4]{0:T(128)S(1)}, s32[4]{0:T(128)S(1)}, bf16[16,384]{1,0:T(8,128)(2,1)S(1)}, bf16[16,128]{1,0:T(8,128)(2,1)S(1)}, bf16[64,6144]{1,0:T(8,128)(2,1)}, /*index=5*/bf16[64,6144]{1,0:T(8,128)(2,1)}, ...), branch_computations={%region_1.2_spmd, %region_2.3_spmd, %region_3.4_spmd} | conditional | bytes 8 | solution.py:390
  5.3 100.6 %layer_flip3.1 = (bf16[16,384]{1,0:T(8,128)(2,1)S(1)}, bf16[16,384]{1,0:T(8,128)(2,1)S(1)}) custom-call(s32[4]{0:T(128)S(1)} %get-tuple-element.56.labels, s32[4]{0:T(128)S(1)} %get-tuple-element.90.freq, bf16[16,384]{1,0:T(8,128)(2,1)S(1)} %get-tuple-element.93.tokens, bf16[16,128]{1,0:T(8,128)(2,1)S(1)} %get-tuple-element.59.share, ...), custom_call_target="tpu_custom_call" | custom-call | tf_op jit(solution)/shard_map/cond/branch_2_fun/layer_flip3/pallas_call | solution.py:374
  106.2 0.6 copy.41
  106.8 0.6 copy.42
  (1 shorter events, 0.0 us)
Async XLA Ops:
  0.6 0.7 copy-start.1
  1.3 3.4 %copy-start = (bf16[16,384]{1,0:T(8,128)(2,1)S(1)}, bf16[16,384]{1,0:T(8,128)(2,1)}, u32[]{:S(2)}) copy-start(bf16[16,384]{1,0:T(8,128)(2,1)} %param.11) | copy-start | bytes 36868
  3.3 0.7 copy-start.3
  4.0 0.7 copy-start.4
  4.7 0.7 copy-start.2

commit v3 on v2

--- a/solution.py
+++ b/solution.py
@@ -14,10 +14,16 @@
 BF16, F32 = jnp.bfloat16, jnp.float32
 ORDER = (0, -1, 1, -2, 2, -3, 3, -4)
 UP_STEPS, DOWN_STEPS = 4, 3
+PAIR_ORDER = {
+    2: ((1, 0, 2, -1, 3, -3, -2, -4), (5, 6, 7, 8, 9, 9, 10, 10)),
+    -2: ((-1, -2, 0, -3, 1, 3, -4, 2), (5, 6, 7, 8, 9, 9, 10, 10)),
+    4: ((2, -2, 1, -3, -1, 3, 0, -4), (7, 7, 8, 8, 9, 9, 10, 10)),
+}
+LAG = 2
 
 
 def kernel(
-    flip, labels, freq, tokens, share, w_gate, w_up, w_down, first_out, second_out,
+    flip, labels, freq, ids, codes, tokens, w_gate, w_up, w_down, first_out, second_out,
     rows, wcat, wd, part, part_in, full, swap, swap_in, hid, ysend, yrecv, yown, xsend, xrecv, fsend, frecv,
     t_loc, w_loc, w_snd, w_rcv, z_snd, z_rcv, up_snd, up_rcv, dn_snd, dn_rcv,
     xr_snd, xr_rcv, xl_snd, xl_rcv, fr_snd, fr_rcv, fl_snd, fl_rcv,
@@ -61,9 +67,19 @@
                 tokens.at[:, pl.ds(i * LANES, LANES)], rows.at[z * planes + i, mine, :], t_loc.at[i]
             )
         )
-    locals_.append(pltpu.make_async_copy(share, rows.at[NZ * planes, mine, :], t_loc.at[planes]))
     for copy in locals_:
         copy.start()
+
+    lane = lax.broadcasted_iota(jnp.int32, (tok_dev, LANES), 1)
+    diag = lax.broadcasted_iota(jnp.int32, (tok_dev, tok_dev), 0) == lax.broadcasted_iota(
+        jnp.int32, (tok_dev, tok_dev), 1
+    )
+    share = jnp.zeros((tok_dev, LANES), F32)
+    for e in range(EXPERTS):
+        line = jnp.sum(jnp.where(ids[...] == e, codes[...].astype(F32) / 256.0, 0.0), axis=0, keepdims=True)
+        column = jnp.sum(jnp.where(diag, jnp.broadcast_to(line, diag.shape), 0.0), axis=1, keepdims=True)
+        share = share + jnp.where(lane == e, column, 0.0)
+    rows[NZ * planes, mine, :] = share.astype(BF16)
 
     barrier = pltpu.get_barrier_semaphore()
     greeted = [at_z(k) for k in range(1, NZ)] + [at_y(k) for k in range(1, NY)]
@@ -176,6 +192,9 @@
             )
             acc = acc + lax.dot_general(lhs, rhs, nt, preferred_element_type=F32)
         part[here, :] = acc
+
+    def to_sibling(k):
+        here = span_of(k)
         send(part.at[here, :], part_in.at[here, :], p_snd.at[k], p_rcv.at[k], sib)
 
     partner_tok = (((expert ^ flip) * 2 + (y % 2)) * NX) + x
@@ -187,17 +206,20 @@
         full[here, :] = both
         swap[here, :] = both.astype(BF16)
 
-    def swap_copy(k):
-        here = span_of(k)
-        g = group(k)
+    def at(off):
+        g = (y + off + NY) % NY
+        return g, pl.ds(pl.multiple_of(g * span, span), span)
+
+    def swap_copy(off):
+        g, here = at(off)
         return remote(swap.at[here, :], swap_in.at[here, :], e_snd.at[g], e_rcv.at[g], (partner_tok, exp))
 
     def to_partner(k):
         @pl.when(core == 1)
         def _():
-            swap_copy(k).start()
-
-    lane = lax.broadcasted_iota(jnp.int32, (1, LANES), 1)
+            swap_copy(ORDER[k]).start()
+
+    lane = lane[:1]
     zero = jnp.zeros((1, LANES), F32)
     freq_v, label_v = zero, jnp.full((1, LANES), -1, jnp.int32)
     own_label = jnp.int32(0)
@@ -213,12 +235,12 @@
     other = jnp.sum(coef * (1.0 - own_lane), axis=1, keepdims=True)
     taken = jnp.where(core == 1, own * member, own_lane)
 
-    def activate(k):
-        here = span_of(k)
+    def activate(off):
+        g, here = at(off)
 
         @pl.when(core == 1)
         def _():
-            swap_copy(k).wait_recv()
+            swap_copy(off).wait_recv()
             v = own * full[here, :] + other * swap_in[here, :].astype(F32)
             full[here, :] = v
 
@@ -226,15 +248,21 @@
         gate, upper = v[:, :units], v[:, units:]
         hid[z, here, :] = (gate / (1.0 + jnp.exp(-gate)) * upper).astype(BF16)
 
-    def along_z(k):
-        here = span_of(k)
+    def along_z(off):
+        g, here = at(off)
         for d in (4, 3, 5, 2, 6, 1, 7):
-            remote(hid.at[z, here, :], hid.at[z, here, :], h_snd.at[k], h_rcv.at[k], at_z(d)).start()
-
-    def finish(k):
-        here = span_of(k)
-        seven = hid.at[pl.ds(0, NZ - 1), here, :]
-        pltpu.make_async_copy(seven, seven, h_rcv.at[k]).wait()
+            remote(hid.at[z, here, :], hid.at[z, here, :], h_snd.at[g], h_rcv.at[g], at_z(d)).start()
+
+    def seven(off):
+        return hid.at[pl.ds(0, NZ - 1), at(off)[1], :]
+
+    def y_copy(off):
+        g, _ = at(off)
+        return remote(ysend.at[g], yrecv.at[y], y_snd.at[g], y_rcv.at[y], (g * NX + x, exp))
+
+    def finish(off):
+        g, here = at(off)
+        pltpu.make_async_copy(seven(off), seven(off), h_rcv.at[g]).wait()
         acc = jnp.zeros((span, 2 * width), F32)
         for j in range(NZ // 2):
             lhs = jnp.concatenate([hid[2 * j, here, :], hid[2 * j + 1, here, :]], axis=1)
@@ -243,58 +271,77 @@
             )
         weight = jnp.sum(rows[NZ * planes, here, :].astype(F32) * taken, axis=1, keepdims=True)
         acc = acc * weight
-        if k == 0:
+        ysend[g] = acc.astype(BF16)
+
+        @pl.when(g == y)
+        def _():
             yown[...] = acc
-        else:
-            ysend[k] = acc.astype(BF16)
-            send(ysend.at[k], yrecv.at[k], y_snd.at[k], y_rcv.at[k], at_y(ORDER[k]))
+
+        @pl.when(g != y)
+        def _():
+            y_copy(off).start()
+
+    if flip == 2:
+        pair_order, pair_step = PAIR_ORDER[4]
+    else:
+        above = (expert % 2 == 0) if flip == 1 else (expert % 2 == 1)
+        pair_step = PAIR_ORDER[2][1]
+        pair_order = [jnp.where(above, a, b) for a, b in zip(PAIR_ORDER[2][0], PAIR_ORDER[-2][0])]
+
+    def both_cores(action, plain, paired):
+        for i in range(max(len(plain), len(paired))):
+            if i < len(plain) and i < len(paired):
+                action(jnp.where(core == 1, paired[i], plain[i]))
+            elif i < len(plain):
+                pl.when(core == 0)(functools.partial(action, plain[i]))
+            else:
+                pl.when(core == 1)(functools.partial(action, paired[i]))
+
+    def due(step):
+        plain = [ORDER[k] for k in range(NY) if k + 2 == step]
+        return plain, [pair_order[k] for k in range(NY) if pair_step[k] == step]
 
     along_y(0)
     along_x(0)
     for copy in loads:
         copy.wait()
-    for k in range(NY):
-        if k + 1 < NY:
-            from_y(k + 1)
-            along_y(k + 1)
-            along_x(k + 1)
-        from_x(k)
+    ahead = 1
+    last = max(pair_step) + LAG
+    for k in range(last + 1):
+        while ahead < NY and ahead <= k + 2:
+            from_y(ahead)
+            along_y(ahead)
+            along_x(ahead)
+            ahead += 1
+        if k < NY:
+            from_x(k)
+        if 0 <= k - 2 < NY:
+            joined(k - 2)
         if k == 1:
             for zz in range(NZ):
                 for which in range(2):
                     i = 2 * zz + which
                     dst = wcat.at[zz, pl.ds(pl.multiple_of(which * units + (1 - core) * half, half), half), :]
                     remote(dst, dst, w_snd.at[i], w_rcv.at[i], sib).wait_recv()
-        if k >= 1:
+        if 0 <= k - 1 < NY:
             from_far(k - 1)
             multiply(k - 1)
-        if k >= 2:
-            joined(k - 2)
-            if k >= 3:
-                to_partner(k - 3)
-    from_far(NY - 1)
-    multiply(NY - 1)
-    joined(NY - 2)
-    to_partner(NY - 3)
-    joined(NY - 1)
-    to_partner(NY - 2)
-    theirs = wd.at[:, pl.ds(pl.multiple_of((1 - core) * width, LANES), width)]
-    remote(theirs, theirs, w_snd.at[2 * NZ], w_rcv.at[2 * NZ], sib).wait_recv()
-    to_partner(NY - 1)
-    for k in range(NY):
-        activate(k)
-        if k >= 1:
-            along_z(k - 1)
-        if k >= 3:
-            finish(k - 3)
-    along_z(NY - 1)
-    for k in range(NY - 3, NY):
-        finish(k)
+        if 0 <= k - 2 < NY:
+            to_partner(k - 2)
+        if k == 2 + LAG:
+            theirs = wd.at[:, pl.ds(pl.multiple_of((1 - core) * width, LANES), width)]
+            remote(theirs, theirs, w_snd.at[2 * NZ], w_rcv.at[2 * NZ], sib).wait_recv()
+        both_cores(finish, *due(k - LAG))
+        both_cores(activate, *due(k))
+        if 0 <= k - 1 < NY:
+            to_sibling(k - 1)
+        both_cores(along_z, *due(k))
 
     acc = yown[...]
     for k in range(1, NY):
-        remote(ysend.at[k], yrecv.at[k], y_snd.at[k], y_rcv.at[k], at_y(ORDER[k])).wait_recv()
-        acc = acc + yrecv[k].astype(F32)
+        g = (y + k) % NY
+        remote(ysend.at[g], yrecv.at[g], y_snd.at[g], y_rcv.at[g], at_y(k)).wait_recv()
+        acc = acc + yrecv[g].astype(F32)
     xsend[...] = acc.astype(BF16).reshape(NX, tok_dev, 2 * width)
     yown[...] = acc
     for k in range(1, NX):
@@ -313,21 +360,19 @@
 
     for copy in zs + gifts + sent:
         copy.wait_send()
-    for k in range(NY):
-        seven = hid.at[pl.ds(0, NZ - 1), span_of(k), :]
-        pltpu.make_async_copy(seven, seven, h_snd.at[k]).wait()
+    for off in range(NY):
+        g, _ = at(off)
+        pltpu.make_async_copy(seven(off), seven(off), h_snd.at[g]).wait()
+        if off > 0:
+            y_copy(off).wait_send()
 
     @pl.when(core == 1)
     def _():
-        for k in range(NY):
-            swap_copy(k).wait_send()
+        for off in range(NY):
+            swap_copy(off).wait_send()
 
 
 def local(tokens, route_ids, gate_codes, merge_labels, freq_counts, w_gate, w_up, w_down):
-    ids = jnp.arange(LANES, dtype=jnp.int32)
-    scale = gate_codes.astype(F32) / 256.0
-    share = jnp.sum(jnp.where(route_ids[:, :, None] == ids, scale[:, :, None], 0.0), axis=1)
-    share = share.astype(BF16)
     tok_dev, width = tokens.shape
     half = w_gate.shape[0]
     count, depth = NX * NY * tok_dev, w_down.shape[0]
@@ -352,7 +397,7 @@
         pltpu.VMEM((NX, tok_dev, 2 * width), BF16),
         pltpu.VMEM((tok_dev, width), BF16),
         pltpu.VMEM((tok_dev, width), BF16),
-        dma((planes + 1,)),
+        dma((planes,)),
         dma((2 * NZ + 1,)),
         dma((2 * NZ + 1,)),
         dma((2 * NZ + 1,)),
@@ -374,23 +419,23 @@
             return pl.pallas_call(
                 functools.partial(kernel, flip),
                 out_shape=(out, out),
-                in_specs=[smem, smem, hbm, hbm, hbm, hbm, hbm],
+                in_specs=[smem, smem, vmem, vmem, hbm, hbm, hbm, hbm],
                 out_specs=(vmem, vmem),
                 scratch_shapes=scratch,
                 compiler_params=pltpu.CompilerParams(
-                    collective_id=flip, has_side_effects=True, vmem_limit_bytes=40 * 1024 * 1024
+                    collective_id=flip, has_side_effects=True, vmem_limit_bytes=60 * 1024 * 1024
                 ),
                 name=f"layer_flip{flip}",
             )(*args)
 
         return run
 
-    same = merge_labels[1:] == merge_labels[0]
-    pairing = jnp.where(same[0], 0, jnp.where(same[1], 1, 2))
+    zero, one, two = (merge_labels[e] for e in range(3))
+    pairing = jnp.where(one == zero, 0, jnp.where(two == zero, 1, 2))
     return lax.switch(
         pairing,
         [variant(1), variant(2), variant(3)],
-        merge_labels, freq_counts, tokens, share, w_gate, w_up, w_down,
+        merge_labels, freq_counts, route_ids.T, gate_codes.T, tokens, w_gate, w_up, w_down,
     )
 
 

time: 106 us -> 92.1 us (0.87); the launches traced: 107 us -> 91.9 us
  Pallas kernels: 101 us -> 84.9 us
  between operations: 1.97 us -> 3.27 us
  local copies, waits for them, and re-layouts: 4.37 us -> 3.25 us
    pallas_call x1, Pallas kernels: 101 us -> 84.9 us  [run(): pl.pallas_call(functools.partial(kernel, flip), out_shape=(out, out), in_...]
    unnamed x12, local copies, waits for them, and re-layouts: 3.78 us -> 1.87 us
where the time goes in v3:
time: 92.1 us; the launch traced here: 91.9 us
  Pallas kernels  84.9 us (92%)
  between operations  3.27 us (4%)
  local copies, waits for them, and re-layouts  3.25 us (4%)
    pallas_call x1, Pallas kernels, run(): pl.pallas_call(functools.partial(kernel, flip), out_shape=(out, out), in_...  84.9 us
    unnamed x12, local copies, waits for them, and re-layouts  1.87 us

profile of v3, /device:TPU:1, one launch (start us, length us, event | category | flops | bytes accessed | tf_op | source)
XLA Modules:
  0.0 91.9 jit_solution(13584396623793515327)
XLA Ops:
  0.6 0.0 copy-start
  0.6 1.4 %fusion = (s32[1]{0:T(128)}, s32[1]{0:T(128)}, s32[1]{0:T(128)}) fusion(s32[4]{0:T(128)} %param.14), kind=kLoop, calls=%fused_computation | loop fusion | bytes 24 | tf_op jit(solution)/shard_map/slice | solution.py:433
  4.6 0.0 copy-start.3
  4.6 0.0 copy-start.1
  4.6 0.0 copy-start.2
  4.6 0.0 copy-start.4
  4.7 0.0 copy-done
  4.7 0.6 copy-done.3
  5.3 0.0 copy-done.1
  5.3 0.0 copy-done.2
  5.3 0.0 copy-done.4
  5.3 85.4 %conditional.1 = ((bf16[16,384]{1,0:T(8,128)(2,1)S(1)}, bf16[16,384]{1,0:T(8,128)(2,1)S(1)})) conditional(s32[]{:T(128)} %bitcast, (s32[4]{0:T(128)S(1)}, s32[4]{0:T(128)S(1)}, s32[2,16]{1,0:T(2,128)S(1)}, s32[2,16]{1,0:T(2,128)S(1)}, bf16[16,384]{1,0:T(8,128)(2,1)S(1)}, /*index=5*/bf16[64,6144]{1,0:T(8,128)(2,1)}, ...), branch_computations={%region_0.1_spmd, %region_1.2_spmd, %region_2.3_spmd} | conditional | bytes 8 | solution.py:435
  5.5 84.9 %layer_flip3.1 = (bf16[16,384]{1,0:T(8,128)(2,1)S(1)}, bf16[16,384]{1,0:T(8,128)(2,1)S(1)}) custom-call(s32[4]{0:T(128)S(1)} %get-tuple-element.64.labels, s32[4]{0:T(128)S(1)} %get-tuple-element.99.freq, s32[2,16]{1,0:T(2,128)S(1)} %get-tuple-element.66.ids, s32[2,16]{1,0:T(2,128)S(1)} %get-tuple-element.67.codes, ...), custom_call_target="tpu_custom_call" | custom-call | tf_op jit(solution)/shard_map/cond/branch_2_fun/layer_flip3/pallas_call | solution.py:419
  90.7 0.6 copy.39
  91.3 0.6 copy.40
Async XLA Ops:
  0.6 4.0 %copy-start = (bf16[16,384]{1,0:T(8,128)(2,1)S(1)}, bf16[16,384]{1,0:T(8,128)(2,1)}, u32[]{:S(2)}) copy-start(bf16[16,384]{1,0:T(8,128)(2,1)} %param.11) | copy-start | bytes 36868
  4.6 0.7 copy-start.3
  4.6 0.7 copy-start.1
  4.6 0.7 copy-start.2
  4.6 0.7 copy-start.4

commit v4 on v3

--- a/solution.py
+++ b/solution.py
@@ -12,22 +12,32 @@
 NX, NY, NZ = 4, 8, 8
 MESH = pl.DeviceIdType.MESH
 BF16, F32 = jnp.bfloat16, jnp.float32
-ORDER = (0, -1, 1, -2, 2, -3, 3, -4)
-UP_STEPS, DOWN_STEPS = 4, 3
-PAIR_ORDER = {
-    2: ((1, 0, 2, -1, 3, -3, -2, -4), (5, 6, 7, 8, 9, 9, 10, 10)),
-    -2: ((-1, -2, 0, -3, 1, 3, -4, 2), (5, 6, 7, 8, 9, 9, 10, 10)),
-    4: ((2, -2, 1, -3, -1, 3, 0, -4), (7, 7, 8, 8, 9, 9, 10, 10)),
+UP_STEPS, DOWN_STEPS = 3, 4
+SIDE = 2
+PLAIN = {
+    2: (0, 1, 2, -1, 3, -2, -4, -3),
+    -2: (0, -1, -2, 1, -3, 2, -4, 3),
+    4: (0, 1, 2, -2, -1, -3, 3, -4),
+    -4: (0, -1, -2, 2, 1, 3, -3, -4),
 }
-LAG = 2
+PAIRED = {
+    2: (1, 0, 2, -1, 3, -2, -4, -3),
+    -2: (-1, -2, 0, -3, 1, -4, 2, 3),
+    4: (2, -2, -1, -3, 1, 3, 0, -4),
+    -4: (-2, 2, 3, 1, -3, -1, -4, 0),
+}
+READY = {2: (1, 2, 2, 4, 4, 6, 6, 7), 4: (2, 3, 5, 5, 6, 6, 7, 7)}
+HOPS = {d: tuple(abs(o) for o in PLAIN[d]) for d in (2, 4)}
+LAG, SUM_LAG = 3, 2
 
 
 def kernel(
-    flip, labels, freq, ids, codes, tokens, w_gate, w_up, w_down, first_out, second_out,
-    rows, wcat, wd, part, part_in, full, swap, swap_in, hid, ysend, yrecv, yown, xsend, xrecv, fsend, frecv,
-    t_loc, w_loc, w_snd, w_rcv, z_snd, z_rcv, up_snd, up_rcv, dn_snd, dn_rcv,
+    flip, labels_hbm, freq_hbm, ids_hbm, codes_hbm, tokens, w_gate, w_up, w_down, first_out, second_out,
+    labels, freq, ids, codes,
+    rows, wcat, wd, part, part_in, full, swap, swap_in, hid, xsend, xrecv, xown, acc_mine, ysend, yrecv, fsend, frecv,
+    s_loc, t_loc, w_loc, w_snd, w_rcv, z_snd, z_rcv, up_snd, up_rcv, dn_snd, dn_rcv,
     xr_snd, xr_rcv, xl_snd, xl_rcv, fr_snd, fr_rcv, fl_snd, fl_rcv,
-    p_snd, p_rcv, e_snd, e_rcv, h_snd, h_rcv, y_snd, y_rcv, x_snd, x_rcv, f_snd, f_rcv,
+    p_snd, p_rcv, e_snd, e_rcv, h_snd, h_rcv, y_snd, y_rcv, x_snd, x_rcv, f_snd, f_rcv, su_snd, su_rcv, sd_snd, sd_rcv,
 ):
     tok, exp = lax.axis_index("tok"), lax.axis_index("exp")
     y, x = tok // NX, tok % NX
@@ -59,6 +69,12 @@
         n = total if n is None else n
         return rows.at[pl.ds(lo, n), pl.ds(pl.multiple_of(t * tok_dev, tok_dev), tok_dev), :]
 
+    barrier = pltpu.get_barrier_semaphore()
+    greeted = [at_z(k) for k in range(1, NZ)] + [at_y(k) for k in range(1, NY)]
+    greeted += [at_x(k) for k in range(1, NX)] + [sib]
+    for dev in greeted:
+        pl.semaphore_signal(barrier, inc=1, device_id=dev, device_id_type=MESH)
+
     mine = pl.ds(pl.multiple_of(tok * tok_dev, tok_dev), tok_dev)
     locals_ = []
     for i in range(planes):
@@ -70,6 +86,24 @@
     for copy in locals_:
         copy.start()
 
+    small = []
+    for i, (src, dst) in enumerate(((ids_hbm, ids), (codes_hbm, codes), (labels_hbm, labels), (freq_hbm, freq))):
+        small.append(pltpu.make_async_copy(src, dst, s_loc.at[i]))
+    for copy in small:
+        copy.start()
+
+    loads = []
+    for zz in range(NZ):
+        for which, ref in enumerate((w_gate, w_up)):
+            dst = wcat.at[zz, pl.ds(pl.multiple_of(which * units + core * half, half), half), :]
+            cols = pl.ds(pl.multiple_of((2 * zz + core) * width, LANES), width)
+            loads.append(pltpu.make_async_copy(ref.at[:, cols], dst, w_loc.at[2 * zz + which]))
+    wide = pl.ds(pl.multiple_of(core * width, LANES), width)
+    loads.append(pltpu.make_async_copy(w_down, wd.at[:, wide], w_loc.at[2 * NZ]))
+    for copy in loads:
+        copy.start()
+    for copy in small:
+        copy.wait()
     lane = lax.broadcasted_iota(jnp.int32, (tok_dev, LANES), 1)
     diag = lax.broadcasted_iota(jnp.int32, (tok_dev, tok_dev), 0) == lax.broadcasted_iota(
         jnp.int32, (tok_dev, tok_dev), 1
@@ -81,22 +115,6 @@
         share = share + jnp.where(lane == e, column, 0.0)
     rows[NZ * planes, mine, :] = share.astype(BF16)
 
-    barrier = pltpu.get_barrier_semaphore()
-    greeted = [at_z(k) for k in range(1, NZ)] + [at_y(k) for k in range(1, NY)]
-    greeted += [at_x(k) for k in range(1, NX)] + [sib]
-    for dev in greeted:
-        pl.semaphore_signal(barrier, inc=1, device_id=dev, device_id_type=MESH)
-
-    loads = []
-    for zz in range(NZ):
-        for which, ref in enumerate((w_gate, w_up)):
-            dst = wcat.at[zz, pl.ds(pl.multiple_of(which * units + core * half, half), half), :]
-            cols = pl.ds(pl.multiple_of((2 * zz + core) * width, LANES), width)
-            loads.append(pltpu.make_async_copy(ref.at[:, cols], dst, w_loc.at[2 * zz + which]))
-    wide = pl.ds(pl.multiple_of(core * width, LANES), width)
-    loads.append(pltpu.make_async_copy(w_down, wd.at[:, wide], w_loc.at[2 * NZ]))
-    for copy in loads:
-        copy.start()
     for copy in locals_:
         copy.wait()
     pl.semaphore_wait(barrier, len(greeted))
@@ -119,12 +137,16 @@
     for copy in gifts:
         copy.start()
 
-    for k in range(1, NZ):
-        got = rows.at[pl.ds(((z - k) % NZ) * planes, planes), mine, :]
-        remote(got, got, z_snd.at[k], z_rcv.at[k], at_z(k)).wait_recv()
+    if flip == 2:
+        above, far = expert < EXPERTS // 2, 4
+    else:
+        above, far = (expert % 2 == 0) if flip == 1 else (expert % 2 == 1), 2
+    plain_order = [jnp.where(above, a, b) for a, b in zip(PLAIN[far], PLAIN[-far])]
+    pair_order = [jnp.where(above, a, b) for a, b in zip(PAIRED[far], PAIRED[-far])]
+    pair_step = [r + 3 for r in READY[far]]
 
     def group(k):
-        return (y + ORDER[k]) % NY
+        return (y + plain_order[k] + NY) % NY
 
     sent = []
 
@@ -133,44 +155,80 @@
         copy.start()
         sent.append(copy)
 
-    def along_y(k):
-        block = rows_of(group(k) * NX + x)
-        off = ORDER[k]
-        if off <= 0 and -off < UP_STEPS:
-            send(block, block, up_snd.at[-off], up_rcv.at[-off], at_y(1))
-        if off >= 0 and off < DOWN_STEPS:
-            send(block, block, dn_snd.at[off], dn_rcv.at[off], at_y(-1))
-
-    def from_y(k):
-        block = rows_of(group(k) * NX + x)
-        off = ORDER[k]
-        if off < 0:
-            remote(block, block, up_snd.at[-off - 1], up_rcv.at[-off - 1], at_y(1)).wait_recv()
-        elif off > 0:
-            remote(block, block, dn_snd.at[off - 1], dn_rcv.at[off - 1], at_y(-1)).wait_recv()
+    side = SIDE * planes
+    main = total - side
+
+    def spread(piece, with_y):
+        for snd, rcv, dev in ((xr_snd, xr_rcv, at_x(1)), (xl_snd, xl_rcv, at_x(-1))):
+            remote(piece, piece, snd.at[0], rcv.at[0], dev).start()
+
+        @pl.when(with_y)
+        def _():
+            for snd, rcv, dev in ((up_snd, up_rcv, at_y(1)), (dn_snd, dn_rcv, at_y(-1))):
+                remote(piece, piece, snd.at[0], rcv.at[0], dev).start()
+
+    def along_y(hop):
+        if hop < UP_STEPS:
+            block = rows_of(((y - hop + NY) % NY) * NX + x, side, main)
+            send(block, block, up_snd.at[hop], up_rcv.at[hop], at_y(1))
+        if hop < DOWN_STEPS:
+            block = rows_of(((y + hop) % NY) * NX + x, side, main)
+            send(block, block, dn_snd.at[hop], dn_rcv.at[hop], at_y(-1))
+
+    def from_y(hop):
+        if hop <= UP_STEPS:
+            block = rows_of(((y - hop + NY) % NY) * NX + x, side, main)
+            remote(block, block, up_snd.at[hop - 1], up_rcv.at[hop - 1], at_y(1)).wait_recv()
+        if hop <= DOWN_STEPS:
+            block = rows_of(((y + hop) % NY) * NX + x, side, main)
+            remote(block, block, dn_snd.at[hop - 1], dn_rcv.at[hop - 1], at_y(-1)).wait_recv()
+
+    def planes_of(k):
+        return (0, total) if k == 0 else (side, main)
 
     def along_x(k):
-        block = rows_of(group(k) * NX + x)
+        block = rows_of(group(k) * NX + x, *planes_of(k))
         send(block, block, xr_snd.at[k], xr_rcv.at[k], at_x(1))
         send(block, block, xl_snd.at[k], xl_rcv.at[k], at_x(-1))
 
-    low = total // 2
+    def pieces(k, t):
+        lo, n = planes_of(k)
+        return rows_of(t, lo, n // 2), rows_of(t, lo + n // 2, n - n // 2)
 
     def from_x(k):
-        left = rows_of(group(k) * NX + (x - 1) % NX)
-        remote(left, left, xr_snd.at[k], xr_rcv.at[k], at_x(1)).wait_recv()
-        piece = rows_of(group(k) * NX + (x - 1) % NX, 0, low)
+        left, right = group(k) * NX + (x + NX - 1) % NX, group(k) * NX + (x + 1) % NX
+        block = rows_of(left, *planes_of(k))
+        remote(block, block, xr_snd.at[k], xr_rcv.at[k], at_x(1)).wait_recv()
+        piece = pieces(k, left)[0]
         send(piece, piece, fr_snd.at[k], fr_rcv.at[k], at_x(1))
-        right = rows_of(group(k) * NX + (x + 1) % NX)
-        remote(right, right, xl_snd.at[k], xl_rcv.at[k], at_x(-1)).wait_recv()
-        piece = rows_of(group(k) * NX + (x + 1) % NX, low, total - low)
+        block = rows_of(right, *planes_of(k))
+        remote(block, block, xl_snd.at[k], xl_rcv.at[k], at_x(-1)).wait_recv()
+        piece = pieces(k, right)[1]
         send(piece, piece, fl_snd.at[k], fl_rcv.at[k], at_x(-1))
 
     def from_far(k):
-        piece = rows_of(group(k) * NX + (x + 2) % NX, 0, low)
-        remote(piece, piece, fr_snd.at[k], fr_rcv.at[k], at_x(1)).wait_recv()
-        piece = rows_of(group(k) * NX + (x + 2) % NX, low, total - low)
-        remote(piece, piece, fl_snd.at[k], fl_rcv.at[k], at_x(-1)).wait_recv()
+        low, high = pieces(k, group(k) * NX + (x + 2) % NX)
+        remote(low, low, fr_snd.at[k], fr_rcv.at[k], at_x(1)).wait_recv()
+        remote(high, high, fl_snd.at[k], fl_rcv.at[k], at_x(-1)).wait_recv()
+
+    def side_block(g):
+        return rows.at[pl.ds(0, side), pl.ds(pl.multiple_of(g * span, span), span), :]
+
+    def side_on(hop):
+        if hop < DOWN_STEPS:
+            block = side_block((y + hop) % NY)
+            send(block, block, sd_snd.at[hop], sd_rcv.at[hop], at_y(-1))
+        if hop < UP_STEPS:
+            block = side_block((y - hop + NY) % NY)
+            send(block, block, su_snd.at[hop], su_rcv.at[hop], at_y(1))
+
+    def side_in(hop):
+        if hop <= UP_STEPS:
+            block = side_block((y - hop + NY) % NY)
+            remote(block, block, su_snd.at[hop - 1], su_rcv.at[hop - 1], at_y(1)).wait_recv()
+        if hop <= DOWN_STEPS:
+            block = side_block((y + hop) % NY)
+            remote(block, block, sd_snd.at[hop - 1], sd_rcv.at[hop - 1], at_y(-1)).wait_recv()
 
     def span_of(k):
         return pl.ds(pl.multiple_of(group(k) * span, span), span)
@@ -217,7 +275,7 @@
     def to_partner(k):
         @pl.when(core == 1)
         def _():
-            swap_copy(ORDER[k]).start()
+            swap_copy(plain_order[k]).start()
 
     lane = lane[:1]
     zero = jnp.zeros((1, LANES), F32)
@@ -256,6 +314,15 @@
     def seven(off):
         return hid.at[pl.ds(0, NZ - 1), at(off)[1], :]
 
+    def x_copy(off, d):
+        g, _ = at(off)
+        there = (x + d) % NX
+        part_rows = pl.ds(pl.multiple_of(there * tok_dev, tok_dev), tok_dev)
+        return remote(xsend.at[g, part_rows, :], xrecv.at[g, NX - d], x_snd.at[g], x_rcv.at[g], at_x(d))
+
+    def three(off):
+        return xrecv.at[at(off)[0], pl.ds(1, NX - 1)]
+
     def y_copy(off):
         g, _ = at(off)
         return remote(ysend.at[g], yrecv.at[y], y_snd.at[g], y_rcv.at[y], (g * NX + x, exp))
@@ -271,22 +338,24 @@
             )
         weight = jnp.sum(rows[NZ * planes, here, :].astype(F32) * taken, axis=1, keepdims=True)
         acc = acc * weight
+        xsend[g] = acc.astype(BF16)
+        acc_mine[...] = acc
+        xown[g] = acc_mine[pl.ds(pl.multiple_of(x * tok_dev, tok_dev), tok_dev), :]
+        for d in (2, 1, 3):
+            x_copy(off, d).start()
+
+    def reduce(off):
+        g, _ = at(off)
+        pltpu.make_async_copy(three(off), three(off), x_rcv.at[g]).wait()
+        acc = xown[g]
+        for d in range(1, NX):
+            acc = acc + xrecv[g, d].astype(F32)
+        xown[g] = acc
         ysend[g] = acc.astype(BF16)
-
-        @pl.when(g == y)
-        def _():
-            yown[...] = acc
 
         @pl.when(g != y)
         def _():
             y_copy(off).start()
-
-    if flip == 2:
-        pair_order, pair_step = PAIR_ORDER[4]
-    else:
-        above = (expert % 2 == 0) if flip == 1 else (expert % 2 == 1)
-        pair_step = PAIR_ORDER[2][1]
-        pair_order = [jnp.where(above, a, b) for a, b in zip(PAIR_ORDER[2][0], PAIR_ORDER[-2][0])]
 
     def both_cores(action, plain, paired):
         for i in range(max(len(plain), len(paired))):
@@ -298,25 +367,49 @@
                 pl.when(core == 1)(functools.partial(action, paired[i]))
 
     def due(step):
-        plain = [ORDER[k] for k in range(NY) if k + 2 == step]
+        plain = [plain_order[k] for k in range(NY) if k + 2 == step]
         return plain, [pair_order[k] for k in range(NY) if pair_step[k] == step]
 
-    along_y(0)
-    along_x(0)
+    spread(rows.at[pl.ds(NZ * planes, 1), mine, :], tok >= 0)
+    spread(own_planes, z >= SIDE)
+    for k in (1, 7, 2, 6, 3, 5, 4):
+        zz = (z - k + NZ) % NZ
+        got = rows.at[pl.ds(zz * planes, planes), mine, :]
+        remote(got, got, z_snd.at[k], z_rcv.at[k], at_z(k)).wait_recv()
+        spread(got, zz >= SIDE)
+    block = rows_of(tok)
+    sent.append(remote(block, block, xr_snd.at[0], xr_rcv.at[0], at_x(1)))
+    sent.append(remote(block, block, xl_snd.at[0], xl_rcv.at[0], at_x(-1)))
+    block = rows_of(tok, side, main)
+    sent.append(remote(block, block, up_snd.at[0], up_rcv.at[0], at_y(1)))
+    sent.append(remote(block, block, dn_snd.at[0], dn_rcv.at[0], at_y(-1)))
     for copy in loads:
         copy.wait()
     ahead = 1
-    last = max(pair_step) + LAG
+    hops = NY // 2
+    last = max(pair_step) + LAG + SUM_LAG
     for k in range(last + 1):
-        while ahead < NY and ahead <= k + 2:
-            from_y(ahead)
-            along_y(ahead)
+        late = k > NY
+        if k + 1 <= hops:
+            from_y(k + 1)
+            along_y(k + 1)
+        while ahead < NY and ahead <= k + 2 and HOPS[far][ahead] <= k + 1:
             along_x(ahead)
             ahead += 1
+        if 0 <= k - 2 < NY:
+            joined(k - 2)
+        if k == 2 + LAG:
+            theirs = wd.at[:, pl.ds(pl.multiple_of((1 - core) * width, LANES), width)]
+            remote(theirs, theirs, w_snd.at[2 * NZ], w_rcv.at[2 * NZ], sib).wait_recv()
+        if not late:
+            both_cores(reduce, *due(k - LAG - SUM_LAG))
+            both_cores(finish, *due(k - LAG))
+        if 0 <= k - 2 < NY:
+            to_partner(k - 2)
+        both_cores(activate, *due(k))
         if k < NY:
             from_x(k)
-        if 0 <= k - 2 < NY:
-            joined(k - 2)
+        both_cores(along_z, *due(k))
         if k == 1:
             for zz in range(NZ):
                 for which in range(2):
@@ -325,31 +418,22 @@
                     remote(dst, dst, w_snd.at[i], w_rcv.at[i], sib).wait_recv()
         if 0 <= k - 1 < NY:
             from_far(k - 1)
+            if k == 1:
+                side_on(0)
+            elif k - 1 <= hops:
+                side_in(k - 1)
+                side_on(k - 1)
             multiply(k - 1)
-        if 0 <= k - 2 < NY:
-            to_partner(k - 2)
-        if k == 2 + LAG:
-            theirs = wd.at[:, pl.ds(pl.multiple_of((1 - core) * width, LANES), width)]
-            remote(theirs, theirs, w_snd.at[2 * NZ], w_rcv.at[2 * NZ], sib).wait_recv()
-        both_cores(finish, *due(k - LAG))
-        both_cores(activate, *due(k))
-        if 0 <= k - 1 < NY:
             to_sibling(k - 1)
-        both_cores(along_z, *due(k))
-
-    acc = yown[...]
+        if late:
+            both_cores(finish, *due(k - LAG))
+            both_cores(reduce, *due(k - LAG - SUM_LAG))
+
+    acc = xown[y]
     for k in range(1, NY):
         g = (y + k) % NY
         remote(ysend.at[g], yrecv.at[g], y_snd.at[g], y_rcv.at[g], at_y(k)).wait_recv()
         acc = acc + yrecv[g].astype(F32)
-    xsend[...] = acc.astype(BF16).reshape(NX, tok_dev, 2 * width)
-    yown[...] = acc
-    for k in range(1, NX):
-        send(xsend.at[(x + k) % NX], xrecv.at[k], x_snd.at[k], x_rcv.at[k], at_x(k))
-    acc = yown[pl.ds(pl.multiple_of(x * tok_dev, tok_dev), tok_dev), :]
-    for k in range(1, NX):
-        remote(xsend.at[0], xrecv.at[k], x_snd.at[k], x_rcv.at[k], at_x(k)).wait_recv()
-        acc = acc + xrecv[k].astype(F32)
     kept = jnp.where(core == 0, acc[:, :width], acc[:, width:]).astype(BF16)
     fsend[...] = jnp.where(core == 0, acc[:, width:], acc[:, :width]).astype(BF16)
     send(fsend, frecv, f_snd, f_rcv, sib)
@@ -363,6 +447,7 @@
     for off in range(NY):
         g, _ = at(off)
         pltpu.make_async_copy(seven(off), seven(off), h_snd.at[g]).wait()
+        pltpu.make_async_copy(three(off), three(off), x_snd.at[g]).wait()
         if off > 0:
             y_copy(off).wait_send()
 
@@ -380,7 +465,12 @@
     planes = width // LANES
     span = NX * tok_dev
     dma = pltpu.SemaphoreType.DMA
+    ids_shape = route_ids.shape[::-1]
     scratch = [
+        pltpu.SMEM((EXPERTS,), jnp.int32),
+        pltpu.SMEM((EXPERTS,), jnp.int32),
+        pltpu.VMEM(ids_shape, jnp.int32),
+        pltpu.VMEM(ids_shape, jnp.int32),
         pltpu.VMEM((NZ * planes + 1, count, LANES), BF16),
         pltpu.VMEM((NZ, 2 * units, width), BF16),
         pltpu.VMEM((depth, 2 * width), BF16),
@@ -391,12 +481,14 @@
         pltpu.VMEM((count, 2 * units), BF16),
         pltpu.VMEM((NZ, count, units), BF16),
         pltpu.VMEM((NY, span, 2 * width), BF16),
-        pltpu.VMEM((NY, span, 2 * width), BF16),
+        pltpu.VMEM((NY, NX, tok_dev, 2 * width), BF16),
+        pltpu.VMEM((NY, tok_dev, 2 * width), F32),
         pltpu.VMEM((span, 2 * width), F32),
-        pltpu.VMEM((NX, tok_dev, 2 * width), BF16),
-        pltpu.VMEM((NX, tok_dev, 2 * width), BF16),
+        pltpu.VMEM((NY, tok_dev, 2 * width), BF16),
+        pltpu.VMEM((NY, tok_dev, 2 * width), BF16),
         pltpu.VMEM((tok_dev, width), BF16),
         pltpu.VMEM((tok_dev, width), BF16),
+        dma((4,)),
         dma((planes,)),
         dma((2 * NZ + 1,)),
         dma((2 * NZ + 1,)),
@@ -405,12 +497,13 @@
         dma((NZ,)),
         *[dma((NY // 2,))] * 4,
         *[dma((NY,))] * 16,
-        dma((NX,)),
-        dma((NX,)),
+        dma((NY,)),
+        dma((NY,)),
         dma(()),
         dma(()),
+        *[dma((NY // 2,))] * 4,
     ]
-    smem, hbm = pl.BlockSpec(memory_space=pltpu.SMEM), pl.BlockSpec(memory_space=pl.ANY)
+    hbm = pl.BlockSpec(memory_space=pltpu.HBM)
     vmem = pl.BlockSpec(memory_space=pltpu.VMEM)
     out = jax.ShapeDtypeStruct((tok_dev, width), BF16)
 
@@ -419,7 +512,7 @@
             return pl.pallas_call(
                 functools.partial(kernel, flip),
                 out_shape=(out, out),
-                in_specs=[smem, smem, vmem, vmem, hbm, hbm, hbm, hbm],
+                in_specs=[hbm] * 8,
                 out_specs=(vmem, vmem),
                 scratch_shapes=scratch,
                 compiler_params=pltpu.CompilerParams(
@@ -430,8 +523,8 @@
 
         return run
 
-    zero, one, two = (merge_labels[e] for e in range(3))
-    pairing = jnp.where(one == zero, 0, jnp.where(two == zero, 1, 2))
+    spot = jnp.maximum(jnp.arange(EXPERTS, dtype=jnp.int32) - 1, 0)
+    pairing = jnp.sum(jnp.where(merge_labels == merge_labels[0], spot, 0))
     return lax.switch(
         pairing,
         [variant(1), variant(2), variant(3)],

time: 92.1 us -> 82.2 us (0.89)
  Pallas kernels: 84.9 us -> 76.5 us
  between operations: 3.27 us -> 1.33 us
    pallas_call x1, Pallas kernels: 84.9 us -> 76.5 us  [run(): pl.pallas_call(functools.partial(kernel, flip), out_shape=(out, out), in_...]
    slice x1 -> x0, local copies, waits for them, and re-layouts: 1.38 us -> none  [local(): zero, one, two = (merge_labels[e] for e in range(3))]
    unnamed x12 -> x10, local copies, waits for them, and re-layouts: 1.87 us -> 2.53 us
where the time goes in v4:
time: 82.2 us; the launch traced here: 82 us
  Pallas kernels  76.5 us (93%)
  local copies, waits for them, and re-layouts  3.23 us (4%)
  between operations  1.33 us (2%)
    pallas_call x1, Pallas kernels, run(): pl.pallas_call(functools.partial(kernel, flip), out_shape=(out, out), in_...  76.5 us
    unnamed x10, local copies, waits for them, and re-layouts  2.53 us

profile of v4, /device:TPU:1, one launch (start us, length us, event | category | flops | bytes accessed | tf_op | source)
XLA Modules:
  0.0 82.0 jit_solution(11300369893355677263)
XLA Ops:
  0.6 0.0 copy-start.5
  0.6 0.6 copy-done.5
  1.3 0.7 fusion
  2.6 0.0 copy-start.4
  2.6 0.0 copy-start.3
  2.6 0.0 copy-start.6
  2.6 0.6 copy-done.4
  3.3 0.0 copy-done.3
  3.3 0.0 copy-done.6
  3.3 77.5 %conditional.1 = ((bf16[16,384]{1,0:T(8,128)(2,1)S(1)}, bf16[16,384]{1,0:T(8,128)(2,1)S(1)})) conditional(s32[]{:T(128)} %clamp.3, (s32[4]{0:T(128)S(1)}, s32[4]{0:T(128)S(1)}, s32[2,16]{1,0:T(2,128)S(1)}, s32[2,16]{1,0:T(2,128)S(1)}, bf16[16,384]{1,0:T(8,128)(2,1)}, /*index=5*/bf16[64,6144]{1,0:T(8,128)(2,1)}, ...), branch_computations={%region_1.2_spmd, %region_2.3_spmd, %region_3.4_spmd} | conditional | bytes 49188 | solution.py:528
  3.3 0.0 copy-start.2
  3.3 0.7 copy-done.2
  4.0 76.5 %layer_flip3.1 = (bf16[16,384]{1,0:T(8,128)(2,1)S(1)}, bf16[16,384]{1,0:T(8,128)(2,1)S(1)}) custom-call(s32[4]{0:T(128)S(1)} %get-tuple-element.64.labels_hbm, s32[4]{0:T(128)S(1)} %get-tuple-element.99.freq_hbm, s32[2,16]{1,0:T(2,128)S(1)} %get-tuple-element.66.ids_hbm, s32[2,16]{1,0:T(2,128)S(1)} %get-tuple-element.67.codes_hbm, ...), custom_call_target="tpu_custom_call" | custom-call | tf_op jit(solution)/shard_map/cond/branch_2_fun/layer_flip3/pallas_call | solution.py:512
  80.8 0.6 copy.39
  81.4 0.6 copy.40
Async XLA Ops:
  0.6 0.7 copy-start.5
  2.6 0.7 copy-start.4
  2.6 0.7 copy-start.3
  2.6 0.7 copy-start.6
  3.3 0.7 copy-start.2

commit v5 on v4

--- a/solution.py
+++ b/solution.py
@@ -12,8 +12,8 @@
 NX, NY, NZ = 4, 8, 8
 MESH = pl.DeviceIdType.MESH
 BF16, F32 = jnp.bfloat16, jnp.float32
-UP_STEPS, DOWN_STEPS = 3, 4
-SIDE = 2
+UP_STEPS, DOWN_STEPS = 4, 3
+SIDE = 1
 PLAIN = {
     2: (0, 1, 2, -1, 3, -2, -4, -3),
     -2: (0, -1, -2, 1, -3, 2, -4, 3),
@@ -92,6 +92,17 @@
     for copy in small:
         copy.start()
 
+    for copy in locals_:
+        copy.wait()
+    pl.semaphore_wait(barrier, len(greeted))
+
+    zs = []
+    own_planes = rows.at[pl.ds(z * planes, planes), mine, :]
+    for k in (4, 3, 5, 2, 6, 1, 7):
+        zs.append(remote(own_planes, own_planes, z_snd.at[k], z_rcv.at[k], at_z(k)))
+    for copy in zs:
+        copy.start()
+
     loads = []
     for zz in range(NZ):
         for which, ref in enumerate((w_gate, w_up)):
@@ -102,6 +113,17 @@
     loads.append(pltpu.make_async_copy(w_down, wd.at[:, wide], w_loc.at[2 * NZ]))
     for copy in loads:
         copy.start()
+    gifts = []
+    for zz in range(NZ):
+        for which, ref in enumerate((w_gate, w_up)):
+            dst = wcat.at[zz, pl.ds(pl.multiple_of(which * units + core * half, half), half), :]
+            cols = pl.ds(pl.multiple_of((2 * zz + (1 - core)) * width, LANES), width)
+            i = 2 * zz + which
+            gifts.append(remote(ref.at[:, cols], dst, w_snd.at[i], w_rcv.at[i], sib))
+    gifts.append(remote(w_down, wd.at[:, wide], w_snd.at[2 * NZ], w_rcv.at[2 * NZ], sib))
+    for copy in gifts:
+        copy.start()
+
     for copy in small:
         copy.wait()
     lane = lax.broadcasted_iota(jnp.int32, (tok_dev, LANES), 1)
@@ -114,28 +136,6 @@
         column = jnp.sum(jnp.where(diag, jnp.broadcast_to(line, diag.shape), 0.0), axis=1, keepdims=True)
         share = share + jnp.where(lane == e, column, 0.0)
     rows[NZ * planes, mine, :] = share.astype(BF16)
-
-    for copy in locals_:
-        copy.wait()
-    pl.semaphore_wait(barrier, len(greeted))
-
-    zs = []
-    own_planes = rows.at[pl.ds(z * planes, planes), mine, :]
-    for k in (1, 7, 2, 6, 3, 5, 4):
-        zs.append(remote(own_planes, own_planes, z_snd.at[k], z_rcv.at[k], at_z(k)))
-    for copy in zs:
-        copy.start()
-
-    gifts = []
-    for zz in range(NZ):
-        for which, ref in enumerate((w_gate, w_up)):
-            dst = wcat.at[zz, pl.ds(pl.multiple_of(which * units + core * half, half), half), :]
-            cols = pl.ds(pl.multiple_of((2 * zz + (1 - core)) * width, LANES), width)
-            i = 2 * zz + which
-            gifts.append(remote(ref.at[:, cols], dst, w_snd.at[i], w_rcv.at[i], sib))
-    gifts.append(remote(w_down, wd.at[:, wide], w_snd.at[2 * NZ], w_rcv.at[2 * NZ], sib))
-    for copy in gifts:
-        copy.start()
 
     if flip == 2:
         above, far = expert < EXPERTS // 2, 4
@@ -516,7 +516,7 @@
                 out_specs=(vmem, vmem),
                 scratch_shapes=scratch,
                 compiler_params=pltpu.CompilerParams(
-                    collective_id=flip, has_side_effects=True, vmem_limit_bytes=60 * 1024 * 1024
+                    collective_id=flip, has_side_effects=True, vmem_limit_bytes=67043328
                 ),
                 name=f"layer_flip{flip}",
             )(*args)

time: 82.2 us -> 81.9 us (level)
    unnamed x10 -> x6, local copies, waits for them, and re-layouts: 2.53 us -> 2.57 us
where the time goes in v5:
time: 81.9 us; the launch traced here: 81.7 us
  Pallas kernels  76.8 us (94%)
  local copies, waits for them, and re-layouts  2.57 us (3%)
  between operations  1.31 us (2%)
    pallas_call x1, Pallas kernels, run(): pl.pallas_call(functools.partial(kernel, flip), out_shape=(out, out), in_...  76.8 us
    unnamed x6, local copies, waits for them, and re-layouts  2.57 us

profile of v5, /device:TPU:1, one launch (start us, length us, event | category | flops | bytes accessed | tf_op | source)
XLA Modules:
  0.0 81.7 jit_solution(5469222727012017308)
XLA Ops:
  0.6 0.0 copy-start.1
  0.6 0.6 copy-done.1
  1.3 0.7 fusion
  2.6 77.1 %conditional.1 = ((bf16[16,384]{1,0:T(8,128)(2,1)}, bf16[16,384]{1,0:T(8,128)(2,1)})) conditional(s32[]{:T(128)} %clamp.3, (s32[4]{0:T(128)}, s32[4]{0:T(128)}, s32[2,16]{1,0:T(2,128)}, s32[2,16]{1,0:T(2,128)}, bf16[16,384]{1,0:T(8,128)(2,1)}, /*index=5*/bf16[64,6144]{1,0:T(8,128)(2,1)}, bf16[64,6144]{1,0:T(8,128)(2,1)}, ...), branch_computations={%region_1.2_spmd, %region_2.3_spmd, %region_3.4_spmd} | conditional | bytes 8 | solution.py:528
  2.6 76.8 %layer_flip1.1 = (bf16[16,384]{1,0:T(8,128)(2,1)}, bf16[16,384]{1,0:T(8,128)(2,1)}) custom-call(s32[4]{0:T(128)} %get-tuple-element.48.labels_hbm, s32[4]{0:T(128)} %get-tuple-element.97.freq_hbm, s32[2,16]{1,0:T(2,128)} %get-tuple-element.50.ids_hbm, s32[2,16]{1,0:T(2,128)} %get-tuple-element.51.codes_hbm, bf16[16,384]{1,0:T(8,128)(2,1)} %get-tuple-element.100.tokens, ...), custom_call_target="tpu_custom_call" | custom-call | tf_op jit(solution)/shard_map/cond/branch_0_fun/layer_flip1/pallas_call | solution.py:512
  79.7 0.0 copy-start
  79.7 1.3 %copy.39 = bf16[16,384]{1,0:T(8,128)(2,1)} copy(bf16[16,384]{1,0:T(8,128)(2,1)} %get-tuple-element.120) | data formatting | bytes 24576
  81.1 0.0 copy-done
  81.1 0.6 copy.40
Async XLA Ops:
  0.6 0.7 copy-start.1
  79.7 1.3 %copy-start = (bf16[16,384]{1,0:T(8,128)(2,1)S(1)}, bf16[16,384]{1,0:T(8,128)(2,1)}, u32[]{:S(2)}) copy-start(bf16[16,384]{1,0:T(8,128)(2,1)} %get-tuple-element.121) | copy-start | bytes 36868
